TPU v7x, 512 devices: a whole 4x4x16 slice. The times are simulated.
512 devices in a mesh: blk: 32 (over z, core), env: 16 (over y, x).
Axes of the slice: x: 4, y: 4, z: 16, core: 2. Of those that a mesh axis runs over, the one named last changes fastest.
Arguments:
- psi: float32 [4096, 1024], P('blk', 'env')
- env_left: bfloat16 [4096, 16, 1024], P('blk', 'env')
- env_right: bfloat16 [16, 1024, 1024], P('env')
- sector_tiles: int32 [16], replicated, may hold values from 1 to 8, as said below
- pairing: int32 [16, 16], replicated, may hold values from 0 to 15, as said below
- coupling: int32 [16, 16], replicated, may hold values from 0 to 1, as said below
Outputs:
- products: float32 [3, 4096, 1024], P(None, 'blk', 'env')
- quotients: float32 [3], replicated
- next_vector: float32 [4096, 1024], P('blk', 'env')
Inputs may be any that keep to these rules, and one draw needn't show every extreme that they name: Sector k covers tiles first_tile[k] to first_tile[k] + sector_tiles[k] - 1 of 128 rows; together the sectors cover all 32 tiles. Channel 0 maps every sector to itself: pairing[k, 0] = k. Channel 0 acts on every sector: coupling[k, 0] = 1.
All inputs are finite; a program needn't handle non-finite values.
Results may differ from a plain program's by a relative error of at most 0.0091.
Values may be sent and summed in bfloat16 or wider, within the bound.
No kernel may reach another device: no remote copies, remote signals or barrier semaphores. Data moves between devices by JAX's collectives and lax.ppermute only.
A program may use at most 64 MiB of HBM per device.

v0:
```python
import jax
import jax.numpy as jnp
from jax import lax
from jax.sharding import PartitionSpec as P

TILE = 128
ITERS = 3


EPSILON = 1e-06


def lookup_sources(sector_tiles, pairing, coupling, tile_ids, source_span):
    first_tile = jnp.cumsum(sector_tiles) - sector_tiles
    sector_ids = jnp.arange(sector_tiles.shape[0], dtype=jnp.int32)
    sector_of = jnp.sum((tile_ids[:, None] >= first_tile[None, :]).astype(jnp.int32), axis=1) - 1
    sector_pick = (sector_of[:, None] == sector_ids[None, :]).astype(jnp.int32)
    source_sector = jnp.sum(sector_pick[:, :, None] * pairing[None, :, :], axis=1)
    coupled = jnp.sum(sector_pick[:, :, None] * coupling[None, :, :], axis=1)
    source_pick = (source_sector[:, :, None] == sector_ids[None, None, :]).astype(jnp.int32)
    source_first = jnp.sum(source_pick * first_tile[None, None, :], axis=2) * TILE
    source_rows = jnp.sum(source_pick * sector_tiles[None, None, :], axis=2) * TILE
    offsets = jnp.arange(source_span, dtype=jnp.int32)
    keep_mask = (offsets[None, None, :] < source_rows[:, :, None]) & (coupled[:, :, None] == 1)
    return (source_first, keep_mask)


def per_device(psi, env_left, env_right, sector_tiles, pairing, coupling):
    row_count, col_width = psi.shape
    env_count = lax.axis_size("env")
    blk_count = lax.axis_size("blk")
    tile_local = row_count // TILE
    source_span = env_left.shape[2]
    local_terms = env_right.shape[0]
    all_terms = pairing.shape[1]
    full_width = col_width * env_count
    tile_ids = lax.axis_index("blk") * tile_local + jnp.arange(tile_local, dtype=jnp.int32)
    source_first, keep_mask = lookup_sources(sector_tiles, pairing, coupling, tile_ids, source_span)
    start_list = jnp.transpose(source_first).reshape(-1)
    term_first = lax.axis_index("env") * local_terms
    local_keep = lax.dynamic_slice_in_dim(keep_mask, term_first, local_terms, 1)
    left_panel = jnp.where(
        local_keep[:, None], env_left.reshape(tile_local, TILE, local_terms, source_span), 0
    )
    entry_count = float(row_count * blk_count * full_width)
    vector = psi
    product_list = []
    quotient_list = []
    for iteration in range(ITERS):
        rounded = vector.astype(jnp.bfloat16)
        every_row = lax.all_gather(rounded, "blk", axis=0, tiled=True)
        padded = jnp.concatenate(
            [every_row, jnp.zeros((source_span, col_width), jnp.bfloat16)], axis=0
        )
        source_slabs = jax.vmap(
            lambda first_row: lax.dynamic_slice_in_dim(padded, first_row, source_span, 0)
        )(start_list)
        source_slabs = source_slabs.reshape(all_terms, tile_local, source_span, col_width)
        moved_rows = lax.all_to_all(source_slabs, "env", split_axis=0, concat_axis=3, tiled=True)
        channel_mix = jnp.einsum(
            "dxtj,tdjc->tdxc", left_panel, moved_rows, preferred_element_type=jnp.float32
        )
        channel_mix = channel_mix.astype(jnp.bfloat16).reshape(local_terms, row_count, full_width)
        partial_sum = jnp.einsum(
            "trb,tbc->rc", channel_mix, env_right, preferred_element_type=jnp.float32
        )
        summed_all = lax.psum(partial_sum, "env")
        product = lax.dynamic_slice_in_dim(
            summed_all, lax.axis_index("env") * col_width, col_width, 1
        )
        inner_sum, square_sum = lax.psum(
            (jnp.sum(vector * product), jnp.sum(vector * vector)), ("blk", "env")
        )
        quotient = inner_sum / square_sum
        residual = product - quotient * vector
        energy = lax.psum(jnp.sum(residual * residual), ("blk", "env"))
        vector = residual * lax.rsqrt(energy / entry_count + EPSILON)
        product_list.append(product)
        quotient_list.append(quotient)
    return (jnp.stack(product_list), jnp.stack(quotient_list), vector)


def solution(mesh):
    placed = (P("blk", "env"), P("blk", "env", None), P("env", None, None), P(), P(), P())
    return jax.shard_map(
        per_device,
        mesh=mesh,
        in_specs=placed,
        out_specs=(P(None, "blk", "env"), P(), P("blk", "env")),
        check_vma=False,
    )
```

profile of v0, /device:TPU:1, one launch (start us, length us, event | category | flops | bytes accessed | tf_op | source)
XLA Modules:
  0.0 1310.4 jit_solution(9975891204792734560)
XLA Ops:
  12.6 39.0 %all_gather.9 = bf16[4096,64]{0,1:T(8,128)(2,1)S(1)} all-gather(bf16[128,64]{0,1:T(8,128)(2,1)S(1)} %convert_element_type.39), channel_id=1, replica_groups=mesh['blk'=32,'env'=16] {'blk'}, dimensions={0}, use_global_device_ids=true | all-gather | bytes 540672 | tf_op jit(solution)/shard_map/all_gather | solution.py:51
  51.6 1.6 broadcast.241.clone2
  53.2 37.1 %while.3 = (s32[]{:T(128)}, bf16[5120,64]{0,1:T(8,128)(2,1)S(1)}, s32[16,2]{0,1:T(2,128)S(1)}, bf16[16,1024,64]{1,2,0:T(8,128)(2,1)}, s32[]{:T(128)}) while((s32[]{:T(128)}, bf16[5120,64]{0,1:T(8,128)(2,1)S(1)}, s32[16,2]{0,1:T(2,128)S(1)}, bf16[16,1024,64]{1,2,0:T(8,128)(2,1)}, s32[]{:T(128)}) %tuple.64), condition=%wide.while_cond, body=%wide.while_body.sunk | while | flops 2 | bytes 1049181 | solution.py:56
  90.3 6.9 all-to-all-start
  99.8 30.3 %all-to-all-done = bf16[16,1,1024,64]{2,3,1,0:T(8,128)(2,1)} async-done(((bf16[16,1,1024,64]{2,3,1,0:T(8,128)(2,1)}), bf16[16,1,1024,64]{2,3,1,0:T(8,128)(2,1)}, u32[]{:S(2)}, u32[]{:S(2)}) %all-to-all-start) | async-done | bytes 2097184 | tf_op jit(solution)/shard_map/all_to_all | solution.py:59
  130.2 3.9 fusion.4
  134.1 107.7 %all-reduce.11.cloned.1.call-done = f32[128,1024]{0,1:T(8,128)} async-done(((f32[128,1024]{0,1:T(8,128)}), f32[128,1024]{0,1:T(8,128)}) %all-reduce.11.cloned.1.call-update) | async-done | bytes 524304 | tf_op jit(solution)/shard_map/psum | solution.py:67
  243.2 105.8 %all-reduce.6 = (f32[]{:T(128)}, f32[]{:T(128)}) all-reduce(f32[]{:T(128)} %get-tuple-element.76, f32[]{:T(128)} %get-tuple-element.75), channel_id=1, replica_groups=mesh['blk'=32,'env'=16] {'blk','env'}, use_global_device_ids=true, to_apply=%region_8.9 | all-reduce | flops 2 | bytes 16 | tf_op jit(solution)/shard_map/psum | solution.py:71
  351.7 99.5 %psum.87 = f32[]{:T(128)} all-reduce(f32[]{:T(128)} %get-tuple-element.113), channel_id=1, replica_groups=mesh['blk'=32,'env'=16] {'blk','env'}, use_global_device_ids=true, to_apply=%region_12.13 | all-reduce | flops 1 | bytes 8 | tf_op jit(solution)/shard_map/psum | solution.py:76
  451.9 29.6 %all_gather.10 = bf16[4096,64]{0,1:T(8,128)(2,1)S(1)} all-gather(bf16[128,64]{0,1:T(8,128)(2,1)S(1)} %multiply_convert_fusion.1), channel_id=1, replica_groups=mesh['blk'=32,'env'=16] {'blk'}, dimensions={0}, use_global_device_ids=true | all-gather | bytes 540672 | tf_op jit(solution)/shard_map/all_gather | solution.py:51
  481.6 1.6 broadcast.241.clone2.1
  483.2 37.2 %while.4 = (s32[]{:T(128)}, bf16[5120,64]{0,1:T(8,128)(2,1)S(1)}, s32[16,2]{0,1:T(2,128)S(1)}, bf16[16,1024,64]{1,2,0:T(8,128)(2,1)}, s32[]{:T(128)}) while((s32[]{:T(128)}, bf16[5120,64]{0,1:T(8,128)(2,1)S(1)}, s32[16,2]{0,1:T(2,128)S(1)}, bf16[16,1024,64]{1,2,0:T(8,128)(2,1)}, s32[]{:T(128)}) %tuple.79), condition=%wide.while_cond.1, body=%wide.while_body.1.sunk | while | flops 2 | bytes 1049181 | solution.py:56
  520.4 32.6 %all_to_all.45 = bf16[16,1,1024,64]{2,3,1,0:T(8,128)(2,1)} all-to-all(bf16[16,1,1024,64]{2,3,1,0:T(8,128)(2,1)} %bitcast.73), channel_id=1, replica_groups=mesh['blk'=32,'env'=16] {'env'}, dimensions={0} | all-to-all | bytes 4194304 | tf_op jit(solution)/shard_map/all_to_all | solution.py:59
  553.0 3.9 fusion.2
  557.0 108.5 %all-reduce.13.cloned.1.call-done = f32[128,1024]{0,1:T(8,128)} async-done(((f32[128,1024]{0,1:T(8,128)}), f32[128,1024]{0,1:T(8,128)}) %all-reduce.13.cloned.1.call-update) | async-done | bytes 524304 | tf_op jit(solution)/shard_map/psum | solution.py:67
  666.9 105.8 %all-reduce.5 = (f32[]{:T(128)}, f32[]{:T(128)}) all-reduce(f32[]{:T(128)} %get-tuple-element.74, f32[]{:T(128)} %get-tuple-element.73), channel_id=1, replica_groups=mesh['blk'=32,'env'=16] {'blk','env'}, use_global_device_ids=true, to_apply=%region_15.16 | all-reduce | flops 2 | bytes 16 | tf_op jit(solution)/shard_map/psum | solution.py:71
  775.4 99.5 %psum.91 = f32[]{:T(128)} all-reduce(f32[]{:T(128)} %get-tuple-element.111), channel_id=1, replica_groups=mesh['blk'=32,'env'=16] {'blk','env'}, use_global_device_ids=true, to_apply=%region_19.20 | all-reduce | flops 1 | bytes 8 | tf_op jit(solution)/shard_map/psum | solution.py:76
  875.7 29.6 %all_gather.11 = bf16[4096,64]{0,1:T(8,128)(2,1)S(1)} all-gather(bf16[128,64]{0,1:T(8,128)(2,1)S(1)} %multiply_convert_fusion), channel_id=1, replica_groups=mesh['blk'=32,'env'=16] {'blk'}, dimensions={0}, use_global_device_ids=true | all-gather | bytes 540672 | tf_op jit(solution)/shard_map/all_gather | solution.py:51
  907.0 39.1 %while.5 = (s32[]{:T(128)}, bf16[5120,64]{0,1:T(8,128)(2,1)S(1)}, s32[16,2]{0,1:T(2,128)S(1)}, bf16[16,1024,64]{1,2,0:T(8,128)(2,1)}, s32[]{:T(128)}) while((s32[]{:T(128)}, bf16[5120,64]{0,1:T(8,128)(2,1)S(1)}, s32[16,2]{0,1:T(2,128)S(1)}, bf16[16,1024,64]{1,2,0:T(8,128)(2,1)}, s32[]{:T(128)}) %tuple.80), condition=%wide.while_cond.2, body=%wide.while_body.2.sunk | while | flops 2 | bytes 1049181 | solution.py:56
  946.1 32.6 %all_to_all.46 = bf16[16,1,1024,64]{2,3,1,0:T(8,128)(2,1)} all-to-all(bf16[16,1,1024,64]{2,3,1,0:T(8,128)(2,1)} %bitcast.71), channel_id=1, replica_groups=mesh['blk'=32,'env'=16] {'env'}, dimensions={0} | all-to-all | bytes 4194304 | tf_op jit(solution)/shard_map/all_to_all | solution.py:59
  978.7 3.9 fusion
  982.6 108.6 %all-reduce.15.cloned.1.call-done = f32[128,1024]{0,1:T(8,128)} async-done(((f32[128,1024]{0,1:T(8,128)}), f32[128,1024]{0,1:T(8,128)}) %all-reduce.15.cloned.1.call-update) | async-done | bytes 524304 | tf_op jit(solution)/shard_map/psum | solution.py:67
  1092.5 105.8 %all-reduce.4 = (f32[]{:T(128)}, f32[]{:T(128)}) all-reduce(f32[]{:T(128)} %get-tuple-element.72, f32[]{:T(128)} %get-tuple-element.71), channel_id=1, replica_groups=mesh['blk'=32,'env'=16] {'blk','env'}, use_global_device_ids=true, to_apply=%region_22.23 | all-reduce | flops 2 | bytes 16 | tf_op jit(solution)/shard_map/psum | solution.py:71
  1201.1 99.5 %psum.95 = f32[]{:T(128)} all-reduce(f32[]{:T(128)} %multiply_reduce_fusion), channel_id=1, replica_groups=mesh['blk'=32,'env'=16] {'blk','env'}, use_global_device_ids=true, to_apply=%region_26.27 | all-reduce | flops 1 | bytes 8 | tf_op jit(solution)/shard_map/psum | solution.py:76
  (330 shorter events, 132.6 us)
Async XLA Ops:
  7.2 123.0 %copy-start = (bf16[1,1024,1024]{2,1,0:T(8,128)(2,1)S(1)}, bf16[1,1024,1024]{2,1,0:T(8,128)(2,1)}, u32[]{:S(2)}) copy-start(bf16[1,1024,1024]{2,1,0:T(8,128)(2,1)} %param.8) | copy-start | bytes 6291460
  90.3 39.8 %copy-start.1 = (bf16[128,1,1024]{2,0,1:T(8,128)(2,1)S(1)}, bf16[128,1,1024]{2,0,1:T(8,128)(2,1)}, u32[]{:S(2)}) copy-start(bf16[128,1,1024]{2,0,1:T(8,128)(2,1)} %param.7) | copy-start | bytes 786436
  90.3 39.8 %all-to-all-start = ((bf16[16,1,1024,64]{2,3,1,0:T(8,128)(2,1)}), bf16[16,1,1024,64]{2,3,1,0:T(8,128)(2,1)}, u32[]{:S(2)}, u32[]{:S(2)}) async-start(bf16[16,1,1024,64]{2,3,1,0:T(8,128)(2,1)} %bitcast.72), calls=%async_computation | async-start | bytes 4194304 | tf_op jit(solution)/shard_map/all_to_all | solution.py:59
  97.3 144.5 %all-reduce.11.cloned.1.call-start = ((), (), s32[]{:S(2)}) async-start(), calls=%async_computation.3 | async-start | bytes 1048576 | tf_op jit(solution)/shard_map/psum | solution.py:67
  130.2 111.6 %copy-start.2 = (f32[128,64]{0,1:T(8,128)S(1)}, f32[128,64]{0,1:T(8,128)}, u32[]{:S(2)}) copy-start(f32[128,64]{0,1:T(8,128)} %param.6) | copy-start | bytes 98308
  134.1 531.4 %all-reduce.13.cloned.1.call-start = ((), (), s32[]{:S(2)}) async-start(), calls=%async_computation.4 | async-start | bytes 1048576 | tf_op jit(solution)/shard_map/psum | solution.py:67
  556.9 534.2 %all-reduce.15.cloned.1.call-start = ((), (), s32[]{:S(2)}) async-start(), calls=%async_computation.5 | async-start | bytes 1048576 | tf_op jit(solution)/shard_map/psum | solution.py:67
Sparse Core Ops, SparseCore 0:
  134.2 107.5 all-reduce.10
  557.1 108.3 all-reduce.12
  982.7 108.4 all-reduce.14
where the time goes:
time: 1310 us
  blocking collectives  779 us (59%)
  waiting for transfers between devices  355 us (27%)
  local copies, waits for them, and re-layouts  119 us (9%)
  between operations  20.6 us (2%)
  other arithmetic  16.2 us (1%)
    psum x3, waiting for transfers between devices, per_device(): summed_all = lax.psum(partial_sum, 'env')  325 us
    psum x3, blocking collectives, per_device(): lax.psum((jnp.sum(vector * product), jnp.sum(vector * vector)), ('blk', '...  317 us
    psum x3, blocking collectives, per_device(): energy = lax.psum(jnp.sum(residual * residual), ('blk', 'env'))  299 us
    gather x288, local copies, waits for them, and re-layouts  112 us
    all_gather x3, blocking collectives, per_device(): every_row = lax.all_gather(rounded, 'blk', axis=0, tiled=True)  98.3 us
    all_to_all x2, blocking collectives, per_device(): lax.all_to_all(source_slabs, 'env', split_axis=0, concat_axis=3, tiled=True)  65.2 us
    all_to_all x1, waiting for transfers between devices, per_device(): lax.all_to_all(source_slabs, 'env', split_axis=0, concat_axis=3, tiled=True)  30.3 us
  transfers between devices with their start and end apart: 4, of which 4 were waited for; matrix products, arithmetic and copies ran while one was open for 0% of the time, Pallas kernels for 0%

commit v1 on v0

v1 whole, which is shorter than its diff:
```python
import functools

import jax
import jax.numpy as jnp
from jax import lax
from jax.experimental import pallas as pl
from jax.experimental.pallas import tpu as pltpu
from jax.sharding import Mesh
from jax.sharding import PartitionSpec as P

TILE = 128
HALF = TILE // 2
ITERS = 3
GROUP = 4

EPSILON = 1e-06

ENV = ("y", "x")
BF16 = jnp.bfloat16
F32 = jnp.float32


def lookup_sources(sector_tiles, pairing, coupling, tile_ids, source_span):
    first_tile = jnp.cumsum(sector_tiles) - sector_tiles
    sector_ids = jnp.arange(sector_tiles.shape[0], dtype=jnp.int32)
    sector_of = jnp.sum((tile_ids[:, None] >= first_tile[None, :]).astype(jnp.int32), axis=1) - 1
    sector_pick = (sector_of[:, None] == sector_ids[None, :]).astype(jnp.int32)
    source_sector = jnp.sum(sector_pick[:, :, None] * pairing[None, :, :], axis=1)
    coupled = jnp.sum(sector_pick[:, :, None] * coupling[None, :, :], axis=1)
    source_pick = (source_sector[:, :, None] == sector_ids[None, None, :]).astype(jnp.int32)
    source_first = jnp.sum(source_pick * first_tile[None, None, :], axis=2) * TILE
    source_rows = jnp.sum(source_pick * sector_tiles[None, None, :], axis=2) * TILE
    offsets = jnp.arange(source_span, dtype=jnp.int32)
    keep_mask = (offsets[None, None, :] < source_rows[:, :, None]) & (coupled[:, :, None] == 1)
    return (source_first, keep_mask)


def pack(block):
    return jnp.concatenate([block[:HALF], block[HALF:]], axis=1)


def unpack(packed):
    width = packed.shape[1] // 2
    return jnp.concatenate([packed[:, :width], packed[:, width:]], axis=0)


def operator_kernel(first, rows, width, *refs):
    if first:
        meta, w_ref, panel_ref, right_ref, out_ref, rows_scr, mix_scr, acc = refs
    else:
        meta, w_ref, p_ref, prev_ref, panel_ref, right_ref, out_ref, rows_scr, mix_scr, acc, q_scr = refs
    step = pl.program_id(0)
    tiles = rows // TILE
    span = panel_ref.shape[2]

    @pl.when(step == 0)
    def _():
        if first:
            d = w_ref[...]
        else:
            w = w_ref[...]
            p = p_ref[...]
            ww = jnp.sum(w * w, keepdims=True)
            wp = jnp.sum(w * p, keepdims=True)
            q = jnp.where(ww > 0, wp / jnp.where(ww > 0, ww, 1.0), 0.0)
            d = p - q * w
            rr = jnp.sum(d * d, keepdims=True)
            lane = lax.broadcasted_iota(jnp.int32, (8, 2 * width), 1)
            q_scr[...] = jnp.where(
                lane == 0, ww, jnp.where(lane == 1, wp, jnp.where(lane == 2, rr, q))
            )
        u = d.astype(BF16)
        core = meta[meta.shape[0] - 1]
        for side in range(2):
            for z in range(tiles // 2):
                block = u[(side * (tiles // 2) + z) * HALF : (side * (tiles // 2) + z + 1) * HALF]
                parity = core if side == 0 else 1 - core
                start = pl.multiple_of((2 * z + parity) * TILE, TILE)
                rows_scr[pl.ds(start, HALF), :] = block[:, :width]
                rows_scr[pl.ds(start + HALF, HALF), :] = block[:, width:]
        rows_scr[pl.ds(rows, span), :] = jnp.zeros((span, width), BF16)
        acc[...] = jnp.zeros_like(acc)

    for i in range(GROUP):
        start = pl.multiple_of(meta[step * GROUP + i], TILE)
        slab = rows_scr[pl.ds(start, span), :]
        mixed = jnp.dot(panel_ref[i], slab, preferred_element_type=F32)
        mix_scr[:, i * width : (i + 1) * width] = mixed.astype(BF16)
    acc[...] += jnp.dot(mix_scr[...], right_ref[...], preferred_element_type=F32)

    @pl.when(step == pl.num_programs(0) - 1)
    def _():
        for e in range(out_ref.shape[0]):
            cols = acc[:, e * width : (e + 1) * width]
            packed = jnp.concatenate([cols[:HALF], cols[HALF:]], axis=1)
            if first:
                out_ref[e, pl.ds(0, HALF), :] = packed
                out_ref[e, pl.ds(HALF, 8), :] = jnp.zeros((8, 2 * width), F32)
            else:
                q = q_scr[0:1, 3:4]
                out_ref[e, pl.ds(0, HALF), :] = packed + q * prev_ref[e]
                out_ref[e, pl.ds(HALF, 8), :] = q_scr[...]


def apply_operator(meta, w, p, prev, panels, right):
    first = p is None
    channels, tile, span = panels.shape
    full = right.shape[1]
    env_count = channels
    width = full // env_count
    rows = w.shape[0] * 2
    whole = lambda shape: pl.BlockSpec(shape, lambda g, m: (0,) * len(shape))
    in_specs = [whole(w.shape)]
    args = [w]
    if not first:
        in_specs += [whole(p.shape), whole(prev.shape)]
        args += [p, prev]
    in_specs += [
        pl.BlockSpec((GROUP, tile, span), lambda g, m: (g, 0, 0)),
        pl.BlockSpec((GROUP * width, full), lambda g, m: (g, 0)),
    ]
    args += [panels, right]
    scratch = [
        pltpu.VMEM((rows + span, width), BF16),
        pltpu.VMEM((tile, GROUP * width), BF16),
        pltpu.VMEM((tile, full), F32),
    ]
    if not first:
        scratch.append(pltpu.VMEM((8, 2 * width), F32))
    out_shape = (env_count, HALF + 8, 2 * width)
    return pl.pallas_call(
        functools.partial(operator_kernel, first, rows, width),
        grid_spec=pltpu.PrefetchScalarGridSpec(
            num_scalar_prefetch=1,
            grid=(channels // GROUP,),
            in_specs=in_specs,
            out_specs=whole(out_shape),
            scratch_shapes=scratch,
        ),
        out_shape=jax.ShapeDtypeStruct(out_shape, F32),
        compiler_params=pltpu.CompilerParams(
            dimension_semantics=("arbitrary",), vmem_limit_bytes=48 * 1024 * 1024
        ),
        cost_estimate=pl.CostEstimate(
            flops=4 * channels * tile * span * width,
            bytes_accessed=panels.size * 2 + right.size * 2 + 3 * 1024 * 1024,
            transcendentals=0,
        ),
        name="operator_first" if first else "operator_next",
    )(meta, *args)


def merge(ww, wp, rr, q):
    ww_all = jnp.sum(ww)
    wp_all = jnp.sum(wp)
    q_all = wp_all / ww_all
    spread = (q - q_all) * jnp.sqrt(ww)
    rr_all = jnp.sum(rr) + jnp.sum(spread * spread)
    return ww_all, wp_all, rr_all, q_all


def gather_rows(packed):
    own = lax.all_gather(packed, "z", axis=0, tiled=True)
    other = lax.ppermute(own, "c", [(0, 1), (1, 0)])
    return jnp.concatenate([own, other], axis=0)


def per_device(psi, env_left, env_right, sector_tiles, pairing, coupling):
    tile, width = psi.shape
    env_count = lax.axis_size(ENV)
    row_count = tile * lax.axis_size(("z", "c"))
    source_span = env_left.shape[2]
    full_width = width * env_count
    entry_count = float(row_count * full_width)
    core = lax.axis_index("c")
    tile_ids = lax.axis_index(("z", "c")).reshape(1)
    source_first, keep_mask = lookup_sources(
        sector_tiles, pairing, coupling, tile_ids, source_span
    )
    meta = jnp.concatenate([source_first.reshape(-1), core.reshape(1)]).astype(jnp.int32)
    local_keep = lax.dynamic_slice_in_dim(keep_mask, lax.axis_index(ENV), 1, 1)
    left_panel = jnp.where(local_keep[0], env_left.reshape(tile, source_span), 0)
    panels = lax.all_gather(left_panel, ENV, axis=0)
    right = lax.all_to_all(
        env_right.reshape(env_count, width, full_width), ENV, 0, 0, tiled=True
    ).reshape(env_count * width, full_width)

    own_w = pack(psi)
    w = gather_rows(own_w)
    sent = apply_operator(meta, w, None, None, panels, right)
    partial = sent[:, :HALF]
    arrived = lax.all_to_all(sent, ENV, 0, 0, tiled=True)
    own_p = jnp.sum(arrived[:, :HALF], axis=0)
    product_list = [own_p]
    quotient_list = []
    for iteration in range(1, ITERS):
        p = gather_rows(own_p)
        sent = apply_operator(meta, w, p, partial, panels, right)
        arrived = lax.all_to_all(sent, ENV, 0, 0, tiled=True)
        notes = arrived[:, HALF]
        _, _, energy, q = merge(notes[:, 0], notes[:, 1], notes[:, 2], notes[:, 3])
        scale = lax.rsqrt(energy / entry_count + EPSILON)
        next_p = scale * (jnp.sum(arrived[:, :HALF], axis=0) - q * own_p)
        own_w = scale * (own_p - q * own_w)
        if iteration < ITERS - 1:
            partial = scale * (sent[:, :HALF] - q * partial)
            w = scale * (p - q * w)
        own_p = next_p
        product_list.append(own_p)
        quotient_list.append(q)

    ww = jnp.sum(own_w * own_w)
    wp = jnp.sum(own_w * own_p)
    q = jnp.where(ww > 0, wp / jnp.where(ww > 0, ww, 1.0), 0.0)
    d = own_p - q * own_w
    rr = jnp.sum(d * d)
    lane = lax.broadcasted_iota(jnp.int32, (8, TILE), 1)

    def note(ww, wp, rr, q):
        return jnp.where(lane == 0, ww, jnp.where(lane == 1, wp, jnp.where(lane == 2, rr, q)))

    def exchange(values, axes):
        count = lax.axis_size(axes)
        sent = jnp.broadcast_to(note(*values)[None], (count, 8, TILE))
        got = lax.all_to_all(sent, axes, 0, 0, tiled=True)[:, 0]
        return merge(got[:, 0], got[:, 1], got[:, 2], got[:, 3])

    values = (ww, wp, rr, q)
    for axes in ("c", ENV, "z"):
        values = exchange(values, axes)
    _, _, energy, q = values
    quotient_list.append(q)
    scale = lax.rsqrt(energy / entry_count + EPSILON)
    own_w = scale * (own_p - q * own_w)
    products = jnp.stack([unpack(x) for x in product_list])
    return (products, jnp.stack(quotient_list), unpack(own_w))


def solution(mesh):
    shape = mesh.devices.shape
    fine = Mesh(mesh.devices.reshape(shape[0] // 2, 2, 4, shape[1] // 4), ("z", "c", "y", "x"))
    blk = ("z", "c")
    placed = (P(blk, ENV), P(blk, ENV, None), P(ENV, None, None), P(), P(), P())
    return jax.shard_map(
        per_device,
        mesh=fine,
        in_specs=placed,
        out_specs=(P(None, blk, ENV), P(), P(blk, ENV)),
        check_vma=False,
    )
```

time: 1310 us -> 314 us (0.24)
  blocking collectives: 779 us -> 119 us
  waiting for transfers between devices: 355 us -> 63.3 us
  local copies, waits for them, and re-layouts: 119 us -> 6.39 us
  starting transfers between devices: 7.06 us -> 51.8 us
  Pallas kernels: 0 us -> 19.1 us
    psum x6 -> x0, blocking collectives: 616 us -> none  [the longest x3 317 us: per_device(): lax.psum((jnp.sum(vector * product), jnp.sum(vector * vector)), ('blk', '...]
    psum x3 -> x0, waiting for transfers between devices: 325 us -> none  [per_device(): summed_all = lax.psum(partial_sum, 'env')]
    gather x288 -> x0, local copies, waits for them, and re-layouts: 112 us -> none
    all_gather x0 -> x1, waiting for transfers between devices: none -> 30.6 us  [per_device(): panels = lax.all_gather(left_panel, ENV, axis=0)]
    all_to_all x2 -> x3, blocking collectives: 65.2 us -> 35.1 us  [the longest x2 30.2 us: per_device(): arrived = lax.all_to_all(sent, ENV, 0, 0, tiled=True)]
    ppermute x0 -> x3, starting transfers between devices: none -> 29.1 us  [gather_rows(): other = lax.ppermute(own, 'c', [(0, 1), (1, 0)])]
    pallas_call x0 -> x3, Pallas kernels: none -> 19.1 us  [apply_operator(): pl.pallas_call(functools.partial(operator_kernel, first, rows, width), gr...]
    all_to_all x1 -> x4, starting transfers between devices: 6.94 us -> 22.6 us  [the longest x2 11.5 us: exchange(): got = lax.all_to_all(sent, axes, 0, 0, tiled=True)[:, 0]]
  transfers between devices with their start and end apart: 4 -> 8, of which waited for: 4 -> 7; matrix products, arithmetic and copies ran while one was open for 0% -> 1% of each run, Pallas kernels for 0% -> 0%
where the time goes in v1:
time: 314 us; the launch traced here: 312 us
  blocking collectives  119 us (38%)
  waiting for transfers between devices  63.3 us (20%)
  starting transfers between devices  51.8 us (16%)
  between operations  30.4 us (10%)
  other arithmetic  22.2 us (7%)
  Pallas kernels  19.1 us (6%)
  local copies, waits for them, and re-layouts  6.39 us (2%)
    all_gather x3, blocking collectives, gather_rows(): own = lax.all_gather(packed, 'z', axis=0, tiled=True)  83.6 us
    all_gather x1, waiting for transfers between devices, per_device(): panels = lax.all_gather(left_panel, ENV, axis=0)  30.6 us
    all_to_all x2, blocking collectives, per_device(): arrived = lax.all_to_all(sent, ENV, 0, 0, tiled=True)  30.2 us
    ppermute x3, starting transfers between devices, gather_rows(): other = lax.ppermute(own, 'c', [(0, 1), (1, 0)])  29.1 us
    pallas_call x3, Pallas kernels, apply_operator(): pl.pallas_call(functools.partial(operator_kernel, first, rows, width), gr...  19.1 us
    all_to_all x2, waiting for transfers between devices, exchange(): got = lax.all_to_all(sent, axes, 0, 0, tiled=True)[:, 0]  17.1 us
    all_to_all x2, starting transfers between devices, exchange(): got = lax.all_to_all(sent, axes, 0, 0, tiled=True)[:, 0]  11.5 us
    all_to_all x1, waiting for transfers between devices, per_device(): arrived = lax.all_to_all(sent, ENV, 0, 0, tiled=True)  11.5 us
  transfers between devices with their start and end apart: 8, of which 7 were waited for; matrix products, arithmetic and copies ran while one was open for 1% of the time, Pallas kernels for 0%

profile of v1, /device:TPU:1, one launch (start us, length us, event | category | flops | bytes accessed | tf_op | source)
XLA Modules:
  0.0 311.9 jit_solution(10373749434071683212)
XLA Ops:
  14.2 1.7 bitcast_select_fusion
  15.9 7.6 %all-to-all-start = ((bf16[16,64,1024]{2,1,0:T(8,128)(2,1)}), bf16[16,64,1024]{2,1,0:T(8,128)(2,1)S(1)}, u32[]{:S(2)}, u32[]{:S(2)}) async-start(bf16[16,64,1024]{2,1,0:T(8,128)(2,1)} %bitcast.23), calls=%async_computation | async-start | bytes 4194304 | tf_op jit(solution)/shard_map/all_to_all | solution.py:184
  23.8 33.3 %all_gather.13 = f32[1024,128]{1,0:T(8,128)S(1)} all-gather(f32[64,128]{1,0:T(8,128)S(1)} %pad_maximum_fusion.3), channel_id=1, replica_groups=mesh['z'=16,'c'=2,'y'=4,'x'=4] {'z'}, dimensions={0}, use_global_device_ids=true | all-gather | bytes 557056 | tf_op jit(solution)/shard_map/all_gather | solution.py:163
  57.1 7.9 %collective-permute-start = (f32[1024,128]{1,0:T(8,128)S(1)}, f32[1024,128]{1,0:T(8,128)S(1)}, u32[]{:S(2)}, u32[]{:S(2)}) collective-permute-start(f32[1024,128]{1,0:T(8,128)S(1)} %all_gather.13), channel_id=1, source_target_pairs={{0,16},{16,0},{1,17},{17,1},{2,18},{18,2},{3,19},{19,3},{4,20},{20... | collective-permute-start | bytes 1572872 | tf_op jit(solution)/shard_map/ppermute | solution.py:164
  65.2 1.4 collective-permute-done
  66.6 30.6 %all-gather.2.cloned.1.call-done.refs_2_.refs_4_ = bf16[16,128,1024]{2,1,0:T(8,128)(2,1)} async-done(((bf16[1,128,1024]{2,1,0:T(8,128)(2,1)}), bf16[16,128,1024]{2,1,0:T(8,128)(2,1)}) %all-gather.2.cloned.1.call-update) | async-done | bytes 4194320 | tf_op jit(solution)/shard_map/all_gather | solution.py:183
  97.1 5.8 %operator_first.1 = f32[16,72,128]{2,1,0:T(8,128)S(1)} custom-call(s32[17]{0:T(128)S(1)} %pad_add_fusion.refs_0_, f32[2048,128]{1,0:T(8,128)S(1)} %constant_dynamic-update-slice_fusion.refs_1_, bf16[16,128,1024]{2,1,0:T(8,128)(2,1)} %all-gather.2.cloned.1.call-done.refs_2_.refs_4_, bf16[1024,1024]{1,0:T(8,128)(2,1)S(1)} %bitcast.20), custom_call_target="tpu_custom_call" | custom-call | flops 536870912 | bytes 9437184 | tf_op jit(solution)/shard_map/operator_first/pallas_call | solution.py:131
  102.9 16.0 %all_to_all.35 = f32[16,72,128]{2,1,0:T(8,128)S(1)} all-to-all(f32[16,72,128]{2,1,0:T(8,128)S(1)} %operator_first.1), channel_id=1, replica_groups=mesh['z'=16,'c'=2,'y'=4,'x'=4] {'y','x'}, dimensions={0} | all-to-all | bytes 1179648 | tf_op jit(solution)/shard_map/all_to_all | solution.py:192
  119.0 26.6 %all_gather.15 = f32[1024,128]{1,0:T(8,128)S(1)} all-gather(f32[64,128]{1,0:T(8,128)S(1)} %slice_reduce_fusion.2), channel_id=1, replica_groups=mesh['z'=16,'c'=2,'y'=4,'x'=4] {'z'}, dimensions={0}, use_global_device_ids=true | all-gather | bytes 557056 | tf_op jit(solution)/shard_map/all_gather | solution.py:163
  145.5 10.8 %collective-permute-start.1 = (f32[1024,128]{1,0:T(8,128)S(1)}, f32[1024,128]{1,0:T(8,128)S(1)}, u32[]{:S(2)}, u32[]{:S(2)}) collective-permute-start(f32[1024,128]{1,0:T(8,128)S(1)} %all_gather.15), channel_id=1, source_target_pairs={{0,16},{16,0},{1,17},{17,1},{2,18},{18,2},{3,19},{19,3},{4,20},{20... | collective-permute-start | bytes 1572872 | tf_op jit(solution)/shard_map/ppermute | solution.py:164
  156.5 1.4 collective-permute-done.1
  158.0 6.3 %operator_next.2 = f32[16,72,128]{2,1,0:T(8,128)S(1)} custom-call(s32[17]{0:T(128)S(1)} %pad_add_fusion.refs_0_, f32[2048,128]{1,0:T(8,128)S(1)} %constant_dynamic-update-slice_fusion.refs_1_, f32[2048,128]{1,0:T(8,128)S(1)} %constant_dynamic-update-slice_fusion.2.refs_2_, f32[16,64,128]{2,1,0:T(8,128)S(1)} %slice.163.refs_3_, ...), custom_call_target="tpu_custom_call" | custom-call | flops 536870912 | bytes 9437184 | tf_op jit(solution)/shard_map/operator_next/pallas_call | solution.py:131
  164.3 14.2 %all_to_all.36 = f32[16,72,128]{2,1,0:T(8,128)S(1)} all-to-all(f32[16,72,128]{2,1,0:T(8,128)S(1)} %operator_next.2), channel_id=1, replica_groups=mesh['z'=16,'c'=2,'y'=4,'x'=4] {'y','x'}, dimensions={0} | all-to-all | bytes 1179648 | tf_op jit(solution)/shard_map/all_to_all | solution.py:199
  183.4 1.4 fusion.refs_3_
  185.9 23.7 %all_gather.16 = f32[1024,128]{1,0:T(8,128)S(1)} all-gather(f32[64,128]{1,0:T(8,128)S(1)} %subtract_multiply_fusion.4), channel_id=1, replica_groups=mesh['z'=16,'c'=2,'y'=4,'x'=4] {'z'}, dimensions={0}, use_global_device_ids=true | all-gather | bytes 557056 | tf_op jit(solution)/shard_map/all_gather | solution.py:163
  209.6 10.4 %collective-permute-start.2 = (f32[1024,128]{1,0:T(8,128)S(1)}, f32[1024,128]{1,0:T(8,128)S(1)}, u32[]{:S(2)}, u32[]{:S(2)}) collective-permute-start(f32[1024,128]{1,0:T(8,128)S(1)} %all_gather.16), channel_id=1, source_target_pairs={{0,16},{16,0},{1,17},{17,1},{2,18},{18,2},{3,19},{19,3},{4,20},{20... | collective-permute-start | bytes 1572872 | tf_op jit(solution)/shard_map/ppermute | solution.py:164
  221.5 7.1 %operator_next.3 = f32[16,72,128]{2,1,0:T(8,128)} custom-call(s32[17]{0:T(128)S(1)} %pad_add_fusion.refs_0_, f32[2048,128]{1,0:T(8,128)S(1)} %subtract_multiply_fusion.refs_1_, f32[2048,128]{1,0:T(8,128)S(1)} %pad_maximum_fusion.refs_2_, f32[16,64,128]{2,1,0:T(8,128)S(1)} %fusion.refs_3_, ...), custom_call_target="tpu_custom_call" | custom-call | flops 536870912 | bytes 9437184 | tf_op jit(solution)/shard_map/operator_next/pallas_call | solution.py:131
  228.6 3.6 %all-to-all-start.3 = ((f32[16,72,128]{2,1,0:T(8,128)}), f32[16,72,128]{2,1,0:T(8,128)S(1)}, u32[]{:S(2)}, u32[]{:S(2)}) async-start(f32[16,72,128]{2,1,0:T(8,128)} %operator_next.3), calls=%async_computation.3 | async-start | bytes 1179648 | tf_op jit(solution)/shard_map/all_to_all | solution.py:199
  232.3 11.5 %all-to-all-done.3 = f32[16,72,128]{2,1,0:T(8,128)S(1)} async-done(((f32[16,72,128]{2,1,0:T(8,128)}), f32[16,72,128]{2,1,0:T(8,128)S(1)}, u32[]{:S(2)}, u32[]{:S(2)}) %all-to-all-start.3) | async-done | bytes 589856 | tf_op jit(solution)/shard_map/all_to_all | solution.py:199
  253.1 4.9 %all_to_all.37 = f32[2,8,128]{2,1,0:T(8,128)S(1)} all-to-all(f32[2,8,128]{2,1,0:T(8,128)S(1)} %broadcast_in_dim.92), channel_id=1, replica_groups=mesh['z'=16,'c'=2,'y'=4,'x'=4] {'c'}, dimensions={0} | all-to-all | bytes 16384 | tf_op jit(solution)/shard_map/all_to_all | solution.py:225
  264.1 3.5 %all-to-all-start.5 = ((f32[16,8,128]{2,1,0:T(8,128)}), f32[16,8,128]{2,1,0:T(8,128)S(1)}, u32[]{:S(2)}, u32[]{:S(2)}) async-start(f32[16,8,128]{2,1,0:T(8,128)} %broadcast_in_dim.97), calls=%async_computation.5 | async-start | bytes 131072 | tf_op jit(solution)/shard_map/all_to_all | solution.py:225
  267.6 6.4 %all-to-all-done.5 = f32[16,8,128]{2,1,0:T(8,128)S(1)} async-done(((f32[16,8,128]{2,1,0:T(8,128)}), f32[16,8,128]{2,1,0:T(8,128)S(1)}, u32[]{:S(2)}, u32[]{:S(2)}) %all-to-all-start.5) | async-done | bytes 65568 | tf_op jit(solution)/shard_map/all_to_all | solution.py:225
  280.1 8.0 %all-to-all-start.6 = ((f32[16,8,128]{2,1,0:T(8,128)}), f32[16,8,128]{2,1,0:T(8,128)S(1)}, u32[]{:S(2)}, u32[]{:S(2)}) async-start(f32[16,8,128]{2,1,0:T(8,128)} %broadcast_in_dim.102), calls=%async_computation.6 | async-start | bytes 131072 | tf_op jit(solution)/shard_map/all_to_all | solution.py:225
  288.9 10.7 %all-to-all-done.6 = f32[16,8,128]{2,1,0:T(8,128)S(1)} async-done(((f32[16,8,128]{2,1,0:T(8,128)}), f32[16,8,128]{2,1,0:T(8,128)S(1)}, u32[]{:S(2)}, u32[]{:S(2)}) %all-to-all-start.6) | async-done | bytes 65568 | tf_op jit(solution)/shard_map/all_to_all | solution.py:225
  (86 shorter events, 26.9 us)
Async XLA Ops:
  7.2 90.0 %all-gather.2.cloned.1.call-start = ((), (), s32[]{:S(2)}) async-start(), calls=%async_computation.7 | async-start | bytes 4456448 | tf_op jit(solution)/shard_map/all_gather | solution.py:183
  15.9 7.6 %copy-start.5 = (f32[128,64]{0,1:T(8,128)S(1)}, f32[128,64]{0,1:T(8,128)}, u32[]{:S(2)}) copy-start(f32[128,64]{0,1:T(8,128)} %param.6) | copy-start | bytes 98308
  15.9 50.7 %all-to-all-start = ((bf16[16,64,1024]{2,1,0:T(8,128)(2,1)}), bf16[16,64,1024]{2,1,0:T(8,128)(2,1)S(1)}, u32[]{:S(2)}, u32[]{:S(2)}) async-start(bf16[16,64,1024]{2,1,0:T(8,128)(2,1)} %bitcast.23), calls=%async_computation | async-start | bytes 4194304 | tf_op jit(solution)/shard_map/all_to_all | solution.py:184
  57.1 9.4 %collective-permute-start = (f32[1024,128]{1,0:T(8,128)S(1)}, f32[1024,128]{1,0:T(8,128)S(1)}, u32[]{:S(2)}, u32[]{:S(2)}) collective-permute-start(f32[1024,128]{1,0:T(8,128)S(1)} %all_gather.13), channel_id=1, source_target_pairs={{0,16},{16,0},{1,17},{17,1},{2,18},{18,2},{3,19},{19,3},{4,20},{20... | collective-permute-start | bytes 1572872 | tf_op jit(solution)/shard_map/ppermute | solution.py:164
  102.9 53.6 %copy-start = (f32[16,72,128]{2,1,0:T(8,128)}, f32[16,72,128]{2,1,0:T(8,128)S(1)}, u32[]{:S(2)}) copy-start(f32[16,72,128]{2,1,0:T(8,128)S(1)} %operator_first.1) | copy-start | bytes 1769476
  145.5 12.4 %collective-permute-start.1 = (f32[1024,128]{1,0:T(8,128)S(1)}, f32[1024,128]{1,0:T(8,128)S(1)}, u32[]{:S(2)}, u32[]{:S(2)}) collective-permute-start(f32[1024,128]{1,0:T(8,128)S(1)} %all_gather.15), channel_id=1, source_target_pairs={{0,16},{16,0},{1,17},{17,1},{2,18},{18,2},{3,19},{19,3},{4,20},{20... | collective-permute-start | bytes 1572872 | tf_op jit(solution)/shard_map/ppermute | solution.py:164
  157.9 6.3 %copy-start.1 = (f32[2048,128]{1,0:T(8,128)}, f32[2048,128]{1,0:T(8,128)S(1)}, u32[]{:S(2)}) copy-start(f32[2048,128]{1,0:T(8,128)S(1)} %constant_dynamic-update-slice_fusion.2.refs_2_) | copy-start | bytes 3145732
  164.3 14.3 %copy-start.3 = (f32[16,72,128]{2,1,0:T(8,128)}, f32[16,72,128]{2,1,0:T(8,128)S(1)}, u32[]{:S(2)}) copy-start(f32[16,72,128]{2,1,0:T(8,128)S(1)} %operator_next.2) | copy-start | bytes 1769476
  178.5 0.8 copy-start.4
  183.4 36.6 %copy-start.2 = (f32[2048,128]{1,0:T(8,128)S(1)}, f32[2048,128]{1,0:T(8,128)}, u32[]{:S(2)}) copy-start(f32[2048,128]{1,0:T(8,128)} %copy-done.1) | copy-start | bytes 3145732
  209.6 11.9 %collective-permute-start.2 = (f32[1024,128]{1,0:T(8,128)S(1)}, f32[1024,128]{1,0:T(8,128)S(1)}, u32[]{:S(2)}, u32[]{:S(2)}) collective-permute-start(f32[1024,128]{1,0:T(8,128)S(1)} %all_gather.16), channel_id=1, source_target_pairs={{0,16},{16,0},{1,17},{17,1},{2,18},{18,2},{3,19},{19,3},{4,20},{20... | collective-permute-start | bytes 1572872 | tf_op jit(solution)/shard_map/ppermute | solution.py:164
  228.6 15.2 %all-to-all-start.3 = ((f32[16,72,128]{2,1,0:T(8,128)}), f32[16,72,128]{2,1,0:T(8,128)S(1)}, u32[]{:S(2)}, u32[]{:S(2)}) async-start(f32[16,72,128]{2,1,0:T(8,128)} %operator_next.3), calls=%async_computation.3 | async-start | bytes 1179648 | tf_op jit(solution)/shard_map/all_to_all | solution.py:199
  264.1 10.0 %all-to-all-start.5 = ((f32[16,8,128]{2,1,0:T(8,128)}), f32[16,8,128]{2,1,0:T(8,128)S(1)}, u32[]{:S(2)}, u32[]{:S(2)}) async-start(f32[16,8,128]{2,1,0:T(8,128)} %broadcast_in_dim.97), calls=%async_computation.5 | async-start | bytes 131072 | tf_op jit(solution)/shard_map/all_to_all | solution.py:225
  280.1 19.6 %all-to-all-start.6 = ((f32[16,8,128]{2,1,0:T(8,128)}), f32[16,8,128]{2,1,0:T(8,128)S(1)}, u32[]{:S(2)}, u32[]{:S(2)}) async-start(f32[16,8,128]{2,1,0:T(8,128)} %broadcast_in_dim.102), calls=%async_computation.6 | async-start | bytes 131072 | tf_op jit(solution)/shard_map/all_to_all | solution.py:225
Sparse Core Ops, SparseCore 0:
  16.0 81.0 all-gather.1

commit v2 on v0

v2 whole, which is shorter than its diff:
```python
import functools

import jax
import jax.numpy as jnp
from jax import lax
from jax.experimental import pallas as pl
from jax.experimental.pallas import tpu as pltpu
from jax.sharding import Mesh
from jax.sharding import PartitionSpec as P

TILE = 128
HALF = TILE // 2
ITERS = 3
GROUP = 4
NOTE = 8

EPSILON = 1e-06

ENV = ("y", "x")
BF16 = jnp.bfloat16
F32 = jnp.float32
PARAMS = dict(vmem_limit_bytes=48 * 1024 * 1024)


def lanes_of(*values):
    lane = lax.broadcasted_iota(jnp.int32, (NOTE, TILE), 1)
    out = jnp.zeros((NOTE, TILE), F32)
    for i, value in enumerate(values):
        out = jnp.where(lane == i, value, out)
    return out


def total(x):
    return jnp.sum(x, keepdims=True)


def own_sums(w, p):
    ww = total(w * w)
    wp = total(w * p)
    q = jnp.where(ww > 0, wp / jnp.where(ww > 0, ww, 1.0), 0.0)
    d = p - q * w
    return d, (ww, wp, total(d * d), q)


def merge(notes):
    ww, wp, rr, q = (notes[:, i : i + 1] for i in range(4))
    ww_all, wp_all = total(ww), total(wp)
    q_all = wp_all / ww_all
    spread = (q - q_all) * jnp.sqrt(ww)
    return ww_all, wp_all, total(rr) + total(spread * spread), q_all


def pack(block):
    return jnp.concatenate([block[:HALF], block[HALF:]], axis=1)


def unpack(packed):
    width = packed.shape[1] // 2
    return jnp.concatenate([packed[:, :width], packed[:, width:]], axis=0)


def smem():
    return pl.BlockSpec(memory_space=pltpu.SMEM)


def vmem():
    return pl.BlockSpec(memory_space=pltpu.VMEM)


def prepare_kernel(place, tiles_ref, pair_ref, couple_ref, left_ref, psi_ref,
                   meta_ref, panel_ref, packed_ref, first):
    sectors, channels = pair_ref.shape
    mine, core, channel = place[0], place[1], place[2]

    def place_sector(k, carry):
        start, sector = carry
        first[k] = start
        sector = jnp.where(start <= mine, k, sector)
        return start + tiles_ref[k], sector

    _, sector = lax.fori_loop(0, sectors, place_sector, (0, 0))
    for t in range(channels):
        meta_ref[t] = first[pair_ref[sector, t]] * TILE
    meta_ref[channels] = core
    source = pair_ref[sector, channel]
    count = jnp.where(couple_ref[sector, channel] == 1, tiles_ref[source] * TILE, 0)
    column = lax.broadcasted_iota(jnp.int32, left_ref.shape, 1)
    panel_ref[...] = jnp.where(column < count, left_ref[...], jnp.zeros((), BF16))
    packed_ref[...] = pack(psi_ref[...])


def prepare(place, sector_tiles, pairing, coupling, left, psi):
    channels = pairing.shape[1]
    return pl.pallas_call(
        prepare_kernel,
        in_specs=[smem()] * 4 + [vmem()] * 2,
        out_specs=[smem(), vmem(), vmem()],
        out_shape=[
            jax.ShapeDtypeStruct((channels + 1,), jnp.int32),
            jax.ShapeDtypeStruct(left.shape, BF16),
            jax.ShapeDtypeStruct((psi.shape[0] // 2, psi.shape[1] * 2), F32),
        ],
        scratch_shapes=[pltpu.SMEM(sector_tiles.shape, jnp.int32)],
        compiler_params=pltpu.CompilerParams(**PARAMS),
        name="prepare",
    )(place, sector_tiles, pairing, coupling, left, psi)


def operator_kernel(turn, rows, width, *refs):
    refs = list(refs)
    meta = refs.pop(0)
    vectors = [(refs.pop(0), refs.pop(0)) for _ in range(turn + 1)]
    earlier = [refs.pop(0) for _ in range(turn)]
    note_ref = refs.pop(0) if turn == 2 else None
    panel_ref, right_ref, out_ref, rows_scr, mix_scr, acc, note_scr = refs
    step = pl.program_id(0)
    pairs = rows // TILE // 2
    span = panel_ref.shape[2]

    @pl.when(step == 0)
    def _():
        def both(index):
            return [ref[...] for ref in vectors[index]]

        if turn == 0:
            d = both(0)
        else:
            w, p = both(0), both(1)
            if turn == 2:
                q0, s0 = note_ref[0:1, 0:1], note_ref[0:1, 1:2]
                w = [s0 * (b - q0 * a) for a, b in zip(w, p)]
                p = both(2)
            ww = total(w[0] * w[0] + w[1] * w[1])
            wp = total(w[0] * p[0] + w[1] * p[1])
            q = jnp.where(ww > 0, wp / jnp.where(ww > 0, ww, 1.0), 0.0)
            d = [b - q * a for a, b in zip(w, p)]
            rr = total(d[0] * d[0] + d[1] * d[1])
            note_scr[...] = lanes_of(ww, wp, rr, q)
        core = meta[meta.shape[0] - 1]
        for side in range(2):
            u = d[side].astype(BF16)
            parity = core if side == 0 else 1 - core
            for z in range(pairs):
                block = u[z * HALF : (z + 1) * HALF]
                start = pl.multiple_of((2 * z + parity) * TILE, TILE)
                rows_scr[pl.ds(start, HALF), :] = block[:, :width]
                rows_scr[pl.ds(start + HALF, HALF), :] = block[:, width:]
        rows_scr[pl.ds(rows, span), :] = jnp.zeros((span, width), BF16)
        acc[...] = jnp.zeros_like(acc)

    for i in range(GROUP):
        start = pl.multiple_of(meta[step * GROUP + i], TILE)
        slab = rows_scr[pl.ds(start, span), :]
        mixed = jnp.dot(panel_ref[i], slab, preferred_element_type=F32)
        mix_scr[:, i * width : (i + 1) * width] = mixed.astype(BF16)
    acc[...] += jnp.dot(mix_scr[...], right_ref[...], preferred_element_type=F32)

    @pl.when(step == pl.num_programs(0) - 1)
    def _():
        for e in range(out_ref.shape[0]):
            cols = acc[:, e * width : (e + 1) * width]
            packed = jnp.concatenate([cols[:HALF], cols[HALF:]], axis=1)
            if turn > 0:
                before = earlier[0][e, pl.ds(0, HALF), :]
                if turn == 2:
                    q0, s0 = note_ref[0:1, 0:1], note_ref[0:1, 1:2]
                    before = s0 * (earlier[1][e, pl.ds(0, HALF), :] - q0 * before)
                packed = packed + note_scr[0:1, 3:4] * before
                out_ref[e, pl.ds(HALF, NOTE), :] = note_scr[...]
            out_ref[e, pl.ds(0, HALF), :] = packed


def apply_operator(meta, vectors, earlier, note, panels, right):
    turn = len(earlier)
    channels, tile, span = panels.shape
    full = right.shape[1]
    width = full // channels
    rows = vectors[0][0].shape[0] * 4
    whole = lambda shape: pl.BlockSpec(shape, lambda g, m: (0,) * len(shape))
    args = [half for vector in vectors for half in vector] + list(earlier)
    if turn == 2:
        args.append(note)
    in_specs = [whole(a.shape) for a in args] + [
        pl.BlockSpec((GROUP, tile, span), lambda g, m: (g, 0, 0)),
        pl.BlockSpec((GROUP * width, full), lambda g, m: (g, 0)),
    ]
    args += [panels, right]
    out_shape = (channels, HALF + (NOTE if turn else 0), 2 * width)
    return pl.pallas_call(
        functools.partial(operator_kernel, turn, rows, width),
        grid_spec=pltpu.PrefetchScalarGridSpec(
            num_scalar_prefetch=1,
            grid=(channels // GROUP,),
            in_specs=in_specs,
            out_specs=whole(out_shape),
            scratch_shapes=[
                pltpu.VMEM((rows + span, width), BF16),
                pltpu.VMEM((tile, GROUP * width), BF16),
                pltpu.VMEM((tile, full), F32),
                pltpu.VMEM((NOTE, TILE), F32),
            ],
        ),
        out_shape=jax.ShapeDtypeStruct(out_shape, F32),
        compiler_params=pltpu.CompilerParams(
            dimension_semantics=("arbitrary",), **PARAMS
        ),
        name=f"operator_{turn}",
    )(meta, *args)


def settle_kernel(entries, last, arrived_ref, p_ref, w_ref, p_out, w_out, note_out, *rest):
    _, _, energy, q = merge(arrived_ref[:, HALF, :])
    scale = lax.rsqrt(energy / entries + EPSILON)
    summed = jnp.sum(arrived_ref[:, pl.ds(0, HALF), :], axis=0)
    p = scale * (summed - q * p_ref[...])
    w = scale * (p_ref[...] - q * w_ref[...])
    p_out[...] = p
    w_out[...] = w
    note_out[...] = lanes_of(q, scale)
    if last:
        _, sums = own_sums(w, p)
        rest[0][...] = jnp.broadcast_to(lanes_of(*sums)[None], rest[0].shape)


def settle(entries, last, arrived, own_p, own_w):
    block = jax.ShapeDtypeStruct(own_p.shape, F32)
    outs = [block, block, jax.ShapeDtypeStruct((NOTE, TILE), F32)]
    if last:
        outs.append(jax.ShapeDtypeStruct((arrived.shape[0], NOTE, TILE), F32))
    return pl.pallas_call(
        functools.partial(settle_kernel, entries, last),
        in_specs=[vmem()] * 3,
        out_specs=[vmem()] * len(outs),
        out_shape=outs,
        compiler_params=pltpu.CompilerParams(**PARAMS),
        name="settle_last" if last else "settle",
    )(arrived, own_p, own_w)


def combine_kernel(got_ref, out_ref):
    note = lanes_of(*merge(got_ref[:, 0, :]))
    out_ref[...] = jnp.broadcast_to(note[None], out_ref.shape)


def combine(got, count):
    return pl.pallas_call(
        combine_kernel,
        in_specs=[vmem()],
        out_specs=vmem(),
        out_shape=jax.ShapeDtypeStruct((count, NOTE, TILE), F32),
        name="combine",
    )(got)


def finish_kernel(entries, own_ref, other_ref, w_ref, note0_ref, note1_ref, *refs):
    product_refs = refs[:ITERS]
    products_out, next_out, quotients_out = refs[ITERS:]
    notes = jnp.concatenate([own_ref[:, 0, :], other_ref[:, 0, :]], axis=0)
    _, _, energy, q = merge(notes)
    scale = lax.rsqrt(energy / entries + EPSILON)
    p = product_refs[ITERS - 1][...]
    next_out[...] = unpack(scale * (p - q * w_ref[...]))
    for n in range(ITERS):
        products_out[n] = unpack(product_refs[n][...])
    quotients_out[...] = lanes_of(note0_ref[0:1, 0:1], note1_ref[0:1, 0:1], q)


def finish(entries, own, other, w, notes, products, tile, width):
    outs = [
        jax.ShapeDtypeStruct((ITERS, tile, width), F32),
        jax.ShapeDtypeStruct((tile, width), F32),
        jax.ShapeDtypeStruct((NOTE, TILE), F32),
    ]
    args = [own, other, w, *notes, *products]
    return pl.pallas_call(
        functools.partial(finish_kernel, entries),
        in_specs=[vmem()] * len(args),
        out_specs=[vmem()] * 3,
        out_shape=outs,
        name="finish",
    )(*args)


def swap(x):
    return lax.ppermute(x, "c", [(0, 1), (1, 0)])


def exchange(x, axes):
    return lax.all_to_all(x, axes, 0, 0, tiled=True)


def gather_rows(packed):
    own = lax.all_gather(packed, "z", axis=0, tiled=True)
    return own, swap(own)


def per_device(psi, env_left, env_right, sector_tiles, pairing, coupling):
    tile, width = psi.shape
    env_count = lax.axis_size(ENV)
    z_count = lax.axis_size("z")
    full_width = width * env_count
    entries = float(tile * z_count * 2 * full_width)
    core = lax.axis_index("c")
    place = jnp.stack([lax.axis_index(("z", "c")), core, lax.axis_index(ENV)]).astype(jnp.int32)
    meta, panel, own_w = prepare(
        place, sector_tiles, pairing, coupling, env_left.reshape(tile, -1), psi
    )
    panels = lax.all_gather(panel, ENV, axis=0)
    w = gather_rows(own_w)

    part = width // 2
    held = env_right.reshape(env_count, 2, part, full_width)
    held = lax.dynamic_index_in_dim(held, core, 1, keepdims=False)
    right_own = exchange(held, ENV)
    right_other = swap(right_own)
    right = jnp.where(
        core == 0,
        jnp.stack([right_own, right_other], axis=1),
        jnp.stack([right_other, right_own], axis=1),
    ).reshape(full_width, full_width)

    sent0 = apply_operator(meta, [w], [], None, panels, right)
    p0_own = jnp.sum(exchange(sent0, ENV), axis=0)
    p0 = gather_rows(p0_own)
    sent1 = apply_operator(meta, [w, p0], [sent0], None, panels, right)
    p1_own, w1_own, note0 = settle(entries, False, exchange(sent1, ENV), p0_own, own_w)
    p1 = gather_rows(p1_own)
    sent2 = apply_operator(meta, [w, p0, p1], [sent0, sent1], note0, panels, right)
    p2_own, w2_own, note1, notes = settle(
        entries, True, exchange(sent2, ENV), p1_own, w1_own
    )
    notes = combine(exchange(notes, ENV), z_count)
    got = exchange(notes, "z")
    products, next_vector, quotients = finish(
        entries, got, swap(got), w2_own, [note0, note1], [p0_own, p1_own, p2_own], tile, width
    )
    return (products, quotients[0, :ITERS], next_vector)


def solution(mesh):
    shape = mesh.devices.shape
    fine = Mesh(mesh.devices.reshape(shape[0] // 2, 2, 4, shape[1] // 4), ("z", "c", "y", "x"))
    blk = ("z", "c")
    placed = (P(blk, ENV), P(blk, ENV, None), P(ENV, None, None), P(), P(), P())
    return jax.shard_map(
        per_device,
        mesh=fine,
        in_specs=placed,
        out_specs=(P(None, blk, ENV), P(), P(blk, ENV)),
        check_vma=False,
    )
```

time: 1310 us -> 286 us (0.22)
  blocking collectives: 779 us -> 178 us
  waiting for transfers between devices: 355 us -> 3.93 us
  local copies, waits for them, and re-layouts: 119 us -> 17 us
  starting transfers between devices: 7.06 us -> 40.8 us
  Pallas kernels: 0 us -> 25.6 us
    psum x6 -> x0, blocking collectives: 616 us -> none  [the longest x3 317 us: per_device(): lax.psum((jnp.sum(vector * product), jnp.sum(vector * vector)), ('blk', '...]
    psum x3 -> x0, waiting for transfers between devices: 325 us -> none  [per_device(): summed_all = lax.psum(partial_sum, 'env')]
    gather x288 -> x0, local copies, waits for them, and re-layouts: 112 us -> none
    ppermute x0 -> x5, starting transfers between devices: none -> 40.8 us  [swap(): return lax.ppermute(x, 'c', [(0, 1), (1, 0)])]
    all_to_all x1 -> x0, waiting for transfers between devices: 30.3 us -> none  [per_device(): lax.all_to_all(source_slabs, 'env', split_axis=0, concat_axis=3, tiled=True)]
    all_to_all x2 -> x6, blocking collectives: 65.2 us -> 94.9 us  [exchange(): return lax.all_to_all(x, axes, 0, 0, tiled=True)]
    pallas_call x0 -> x8, Pallas kernels: none -> 25.6 us  [the longest x3 18.9 us: apply_operator(): pl.pallas_call(functools.partial(operator_kernel, turn, rows, width), gri...]
    all_gather x3, blocking collectives: 98.3 us -> 82.7 us  [gather_rows(): own = lax.all_gather(packed, 'z', axis=0, tiled=True)]
  transfers between devices with their start and end apart: 4 -> 6, of which waited for: 4 -> 3; matrix products, arithmetic and copies ran while one was open for 0% -> 1% of each run, Pallas kernels for 0% -> 0%
where the time goes in v2:
time: 286 us; the launch traced here: 285 us
  blocking collectives  178 us (62%)
  starting transfers between devices  40.8 us (14%)
  Pallas kernels  25.6 us (9%)
  local copies, waits for them, and re-layouts  17 us (6%)
  between operations  14.3 us (5%)
  other arithmetic  5.22 us (2%)
  waiting for transfers between devices  3.93 us (1%)
    all_to_all x6, blocking collectives, exchange(): return lax.all_to_all(x, axes, 0, 0, tiled=True)  94.9 us
    all_gather x3, blocking collectives, gather_rows(): own = lax.all_gather(packed, 'z', axis=0, tiled=True)  82.7 us
    ppermute x5, starting transfers between devices, swap(): return lax.ppermute(x, 'c', [(0, 1), (1, 0)])  40.8 us
    pallas_call x3, Pallas kernels, apply_operator(): pl.pallas_call(functools.partial(operator_kernel, turn, rows, width), gri...  18.9 us
    unnamed x41, local copies, waits for them, and re-layouts  15.7 us
  transfers between devices with their start and end apart: 6, of which 3 were waited for; matrix products, arithmetic and copies ran while one was open for 1% of the time, Pallas kernels for 0%

profile of v2, /device:TPU:1, one launch (start us, length us, event | category | flops | bytes accessed | tf_op | source)
XLA Modules:
  0.0 284.6 jit_solution(1157222740659432063)
XLA Ops:
  11.3 1.8 prepare.1
  13.2 22.1 %all_to_all.30 = bf16[16,32,1024]{2,1,0:T(8,128)(2,1)} all-to-all(bf16[16,32,1024]{2,1,0:T(8,128)(2,1)S(1)} %dynamic-slice_bitcast_fusion), channel_id=1, replica_groups=mesh['z'=16,'c'=2,'y'=4,'x'=4] {'y','x'}, dimensions={0} | all-to-all | bytes 2097152 | tf_op jit(solution)/shard_map/all_to_all | solution.py:289
  35.4 5.4 %collective-permute-start.1 = (bf16[16,32,1024]{2,1,0:T(8,128)(2,1)}, bf16[16,32,1024]{2,1,0:T(8,128)(2,1)}, u32[]{:S(2)}, u32[]{:S(2)}) collective-permute-start(bf16[16,32,1024]{2,1,0:T(8,128)(2,1)} %all_to_all.30), channel_id=1, source_target_pairs={{0,16},{16,0},{1,17},{17,1},{2,18},{18,2},{3,19},{19,3},{4,20},{20... | collective-permute-start | bytes 3145736 | tf_op jit(solution)/shard_map/ppermute | solution.py:285
  40.8 33.5 %all_gather.15.refs_1_ = f32[1024,128]{1,0:T(8,128)S(1)} all-gather(f32[64,128]{1,0:T(8,128)S(1)} %get-tuple-element.17.w_ref), channel_id=1, replica_groups=mesh['z'=16,'c'=2,'y'=4,'x'=4] {'z'}, dimensions={0}, use_global_device_ids=true | all-gather | bytes 557056 | tf_op jit(solution)/shard_map/all_gather | solution.py:293
  74.3 8.1 %collective-permute-start = (f32[1024,128]{1,0:T(8,128)S(1)}, f32[1024,128]{1,0:T(8,128)S(1)}, u32[]{:S(2)}, u32[]{:S(2)}) collective-permute-start(f32[1024,128]{1,0:T(8,128)S(1)} %all_gather.15.refs_1_), channel_id=1, source_target_pairs={{0,16},{16,0},{1,17},{17,1},{2,18},{18,2},{3,19},{19,3},{4,20},{20... | collective-permute-start | bytes 1572872 | tf_op jit(solution)/shard_map/ppermute | solution.py:285
  82.4 4.1 %maximum_select_fusion = bf16[16,2,32,1024]{3,2,1,0:T(8,128)(2,1)} fusion(bf16[16,1,32,1024]{3,2,1,0:T(8,128)(2,1)} %bitcast.8, bf16[16,1,32,1024]{3,2,1,0:T(8,128)(2,1)} %bitcast.7, pred[]{:T(512)S(6)} %eq.3), kind=kLoop, calls=%fused_computation | loop fusion | flops 3145728 | bytes 4194305 | tf_op jit(solution)/shard_map/jit(_where)/select_n | solution.py:316
  87.3 1.6 copy-done.1
  89.9 5.8 %operator_0.1.refs_5_.refs_7_ = f32[16,64,128]{2,1,0:T(8,128)S(1)} custom-call(s32[17]{0:T(128)S(1)} %get-tuple-element.16.refs_0_, f32[1024,128]{1,0:T(8,128)S(1)} %all_gather.15.refs_1_, f32[1024,128]{1,0:T(8,128)S(1)} %copy-done.4, bf16[16,128,1024]{2,1,0:T(8,128)(2,1)} %bitcast.18, bf16[1024,1024]{1,0:T(8,128)(2,1)S(1)} %bitcast.15), custom_call_target="tpu_custom_call" | custom-call | tf_op jit(solution)/shard_map/operator_0/pallas_call | solution.py:189
  95.7 14.1 %all_to_all.31 = f32[16,64,128]{2,1,0:T(8,128)} all-to-all(f32[16,64,128]{2,1,0:T(8,128)S(1)} %operator_0.1.refs_5_.refs_7_), channel_id=1, replica_groups=mesh['z'=16,'c'=2,'y'=4,'x'=4] {'y','x'}, dimensions={0} | all-to-all | bytes 1048576 | tf_op jit(solution)/shard_map/all_to_all | solution.py:289
  110.9 25.8 %all_gather.18.refs_3_ = f32[1024,128]{1,0:T(8,128)S(1)} all-gather(f32[64,128]{1,0:T(8,128)S(1)} %reduce_sum.9.p_ref.refs_0_), channel_id=1, replica_groups=mesh['z'=16,'c'=2,'y'=4,'x'=4] {'z'}, dimensions={0}, use_global_device_ids=true | all-gather | bytes 557056 | tf_op jit(solution)/shard_map/all_gather | solution.py:293
  136.7 10.8 %collective-permute-start.2 = (f32[1024,128]{1,0:T(8,128)S(1)}, f32[1024,128]{1,0:T(8,128)S(1)}, u32[]{:S(2)}, u32[]{:S(2)}) collective-permute-start(f32[1024,128]{1,0:T(8,128)S(1)} %all_gather.18.refs_3_), channel_id=1, source_target_pairs={{0,16},{16,0},{1,17},{17,1},{2,18},{18,2},{3,19},{19,3},{4,20},{20... | collective-permute-start | bytes 1572872 | tf_op jit(solution)/shard_map/ppermute | solution.py:285
  149.0 1.6 copy-done.2
  151.6 6.2 %operator_1.1.refs_8_ = f32[16,72,128]{2,1,0:T(8,128)S(1)} custom-call(s32[17]{0:T(128)S(1)} %get-tuple-element.16.refs_0_, f32[1024,128]{1,0:T(8,128)S(1)} %all_gather.15.refs_1_, f32[1024,128]{1,0:T(8,128)S(1)} %copy-done.5, f32[1024,128]{1,0:T(8,128)S(1)} %all_gather.18.refs_3_, f32[1024,128]{1,0:T(8,128)S(1)} %collective-permute-done.2.refs_4_, ...), custom_call_target="tpu_custom_call" | custom-call | tf_op jit(solution)/shard_map/operator_1/pallas_call | solution.py:189
  157.9 14.4 %all_to_all.32.arrived_ref = f32[16,72,128]{2,1,0:T(8,128)S(1)} all-to-all(f32[16,72,128]{2,1,0:T(8,128)S(1)} %operator_1.1.refs_8_), channel_id=1, replica_groups=mesh['z'=16,'c'=2,'y'=4,'x'=4] {'y','x'}, dimensions={0} | all-to-all | bytes 1179648 | tf_op jit(solution)/shard_map/all_to_all | solution.py:289
  172.7 23.5 %all_gather.19.refs_5_ = f32[1024,128]{1,0:T(8,128)S(1)} all-gather(f32[64,128]{1,0:T(8,128)S(1)} %get-tuple-element.19.p_ref.refs_1_), channel_id=1, replica_groups=mesh['z'=16,'c'=2,'y'=4,'x'=4] {'z'}, dimensions={0}, use_global_device_ids=true | all-gather | bytes 557056 | tf_op jit(solution)/shard_map/all_gather | solution.py:293
  196.2 10.2 %collective-permute-start.3 = (f32[1024,128]{1,0:T(8,128)S(1)}, f32[1024,128]{1,0:T(8,128)S(1)}, u32[]{:S(2)}, u32[]{:S(2)}) collective-permute-start(f32[1024,128]{1,0:T(8,128)S(1)} %all_gather.19.refs_5_), channel_id=1, source_target_pairs={{0,16},{16,0},{1,17},{17,1},{2,18},{18,2},{3,19},{19,3},{4,20},{20... | collective-permute-start | bytes 1572872 | tf_op jit(solution)/shard_map/ppermute | solution.py:285
  207.9 6.9 %operator_2.1 = f32[16,72,128]{2,1,0:T(8,128)S(1)} custom-call(s32[17]{0:T(128)S(1)} %get-tuple-element.16.refs_0_, f32[1024,128]{1,0:T(8,128)S(1)} %all_gather.15.refs_1_, f32[1024,128]{1,0:T(8,128)S(1)} %copy-done.6, f32[1024,128]{1,0:T(8,128)S(1)} %all_gather.18.refs_3_, f32[1024,128]{1,0:T(8,128)S(1)} %collective-permute-done.2.refs_4_, ...), custom_call_target="tpu_custom_call" | custom-call | tf_op jit(solution)/shard_map/operator_2/pallas_call | solution.py:189
  214.8 14.2 %all_to_all.33.arrived_ref = f32[16,72,128]{2,1,0:T(8,128)S(1)} all-to-all(f32[16,72,128]{2,1,0:T(8,128)S(1)} %operator_2.1), channel_id=1, replica_groups=mesh['z'=16,'c'=2,'y'=4,'x'=4] {'y','x'}, dimensions={0} | all-to-all | bytes 1179648 | tf_op jit(solution)/shard_map/all_to_all | solution.py:289
  231.4 9.8 %all_to_all.34.got_ref = f32[16,8,128]{2,1,0:T(8,128)} all-to-all(f32[16,8,128]{2,1,0:T(8,128)S(1)} %get-tuple-element.22), channel_id=1, replica_groups=mesh['z'=16,'c'=2,'y'=4,'x'=4] {'y','x'}, dimensions={0} | all-to-all | bytes 131072 | tf_op jit(solution)/shard_map/all_to_all | solution.py:289
  241.3 1.9 combine.1
  243.1 20.3 %all_to_all.35.own_ref = f32[16,8,128]{2,1,0:T(8,128)S(1)} all-to-all(f32[16,8,128]{2,1,0:T(8,128)} %combine.1), channel_id=1, replica_groups=mesh['z'=16,'c'=2,'y'=4,'x'=4] {'z'}, dimensions={0} | all-to-all | bytes 131072 | tf_op jit(solution)/shard_map/all_to_all | solution.py:289
  263.4 6.3 %collective-permute-start.4 = (f32[16,8,128]{2,1,0:T(8,128)S(1)}, f32[16,8,128]{2,1,0:T(8,128)S(1)}, u32[]{:S(2)}, u32[]{:S(2)}) collective-permute-start(f32[16,8,128]{2,1,0:T(8,128)S(1)} %all_to_all.35.own_ref), channel_id=1, source_target_pairs={{0,16},{16,0},{1,17},{17,1},{2,18},{18,2},{3,19},{19,3},{4,20},{20... | collective-permute-start | bytes 196616 | tf_op jit(solution)/shard_map/ppermute | solution.py:285
  271.2 2.1 finish.1
  273.3 1.7 copy.10
  (52 shorter events, 18.3 us)
Async XLA Ops:
  7.2 5.9 %copy-start = (bf16[1,1024,1024]{2,1,0:T(8,128)(2,1)S(1)}, bf16[1,1024,1024]{2,1,0:T(8,128)(2,1)}, u32[]{:S(2)}) copy-start(bf16[1,1024,1024]{2,1,0:T(8,128)(2,1)} %param.8) | copy-start | bytes 6291460
  7.2 80.1 %all-gather.3.cloned.1.call-start = ((), (), s32[]{:S(2)}) async-start(), calls=%async_computation.6 | async-start | bytes 4456448 | tf_op jit(solution)/shard_map/all_gather | solution.py:308
  8.3 1.0 copy-start.9
  9.3 0.7 copy-start.13
  10.0 0.7 copy-start.14
  10.7 0.7 copy-start.16
  35.4 47.0 %collective-permute-start.1 = (bf16[16,32,1024]{2,1,0:T(8,128)(2,1)}, bf16[16,32,1024]{2,1,0:T(8,128)(2,1)}, u32[]{:S(2)}, u32[]{:S(2)}) collective-permute-start(bf16[16,32,1024]{2,1,0:T(8,128)(2,1)} %all_to_all.30), channel_id=1, source_target_pairs={{0,16},{16,0},{1,17},{17,1},{2,18},{18,2},{3,19},{19,3},{4,20},{20... | collective-permute-start | bytes 3145736 | tf_op jit(solution)/shard_map/ppermute | solution.py:285
  74.3 12.2 %collective-permute-start = (f32[1024,128]{1,0:T(8,128)S(1)}, f32[1024,128]{1,0:T(8,128)S(1)}, u32[]{:S(2)}, u32[]{:S(2)}) collective-permute-start(f32[1024,128]{1,0:T(8,128)S(1)} %all_gather.15.refs_1_), channel_id=1, source_target_pairs={{0,16},{16,0},{1,17},{17,1},{2,18},{18,2},{3,19},{19,3},{4,20},{20... | collective-permute-start | bytes 1572872 | tf_op jit(solution)/shard_map/ppermute | solution.py:285
  86.5 0.8 copy-start.3
  87.3 1.6 copy-start.1
  88.9 1.0 copy-start.4
  110.9 61.4 %copy-start.7 = (f32[64,128]{1,0:T(8,128)}, f32[64,128]{1,0:T(8,128)S(1)}, u32[]{:S(2)}) copy-start(f32[64,128]{1,0:T(8,128)S(1)} %reduce_sum.9.p_ref.refs_0_) | copy-start | bytes 98308
  136.7 12.3 %collective-permute-start.2 = (f32[1024,128]{1,0:T(8,128)S(1)}, f32[1024,128]{1,0:T(8,128)S(1)}, u32[]{:S(2)}, u32[]{:S(2)}) collective-permute-start(f32[1024,128]{1,0:T(8,128)S(1)} %all_gather.18.refs_3_), channel_id=1, source_target_pairs={{0,16},{16,0},{1,17},{17,1},{2,18},{18,2},{3,19},{19,3},{4,20},{20... | collective-permute-start | bytes 1572872 | tf_op jit(solution)/shard_map/ppermute | solution.py:285
  149.0 1.6 copy-start.2
  150.6 1.0 copy-start.5
  157.9 50.0 %copy-start.6 = (f32[1024,128]{1,0:T(8,128)S(1)}, f32[1024,128]{1,0:T(8,128)}, u32[]{:S(2)}) copy-start(f32[1024,128]{1,0:T(8,128)} %copy-done.3) | copy-start | bytes 1572868
  172.7 42.1 %copy-start.12 = (f32[8,128]{1,0:T(8,128)}, f32[8,128]{1,0:T(8,128)S(1)}, u32[]{:S(2)}) copy-start(f32[8,128]{1,0:T(8,128)S(1)} %get-tuple-element.20.refs_9_.note0_ref) | copy-start | bytes 12292
  172.7 56.3 %copy-start.8 = (f32[64,128]{1,0:T(8,128)}, f32[64,128]{1,0:T(8,128)S(1)}, u32[]{:S(2)}) copy-start(f32[64,128]{1,0:T(8,128)S(1)} %get-tuple-element.19.p_ref.refs_1_) | copy-start | bytes 98308
  196.2 11.7 %collective-permute-start.3 = (f32[1024,128]{1,0:T(8,128)S(1)}, f32[1024,128]{1,0:T(8,128)S(1)}, u32[]{:S(2)}, u32[]{:S(2)}) collective-permute-start(f32[1024,128]{1,0:T(8,128)S(1)} %all_gather.19.refs_5_), channel_id=1, source_target_pairs={{0,16},{16,0},{1,17},{17,1},{2,18},{18,2},{3,19},{19,3},{4,20},{20... | collective-permute-start | bytes 1572872 | tf_op jit(solution)/shard_map/ppermute | solution.py:285
  229.6 0.6 copy-start.10
  230.2 0.6 copy-start.11
  263.4 7.2 %copy-start.17 = (f32[16,8,128]{2,1,0:T(8,128)}, f32[16,8,128]{2,1,0:T(8,128)S(1)}, u32[]{:S(2)}) copy-start(f32[16,8,128]{2,1,0:T(8,128)S(1)} %all_to_all.35.own_ref) | copy-start | bytes 196612
  263.4 7.2 %collective-permute-start.4 = (f32[16,8,128]{2,1,0:T(8,128)S(1)}, f32[16,8,128]{2,1,0:T(8,128)S(1)}, u32[]{:S(2)}, u32[]{:S(2)}) collective-permute-start(f32[16,8,128]{2,1,0:T(8,128)S(1)} %all_to_all.35.own_ref), channel_id=1, source_target_pairs={{0,16},{16,0},{1,17},{17,1},{2,18},{18,2},{3,19},{19,3},{4,20},{20... | collective-permute-start | bytes 196616 | tf_op jit(solution)/shard_map/ppermute | solution.py:285
  270.6 0.6 copy-start.18
  (1 other events, 0.6 us)
Sparse Core Ops, SparseCore 0:
  13.2 71.8 all-gather.2

commit v3 on v2

--- a/solution.py
+++ b/solution.py
@@ -13,6 +13,7 @@
 ITERS = 3
 GROUP = 4
 NOTE = 8
+TAIL = 16
 
 EPSILON = 1e-06
 
@@ -34,12 +35,22 @@
     return jnp.sum(x, keepdims=True)
 
 
+def quotient_of(ww, wp):
+    return jnp.where(ww > 0, wp / jnp.where(ww > 0, ww, 1.0), 0.0)
+
+
 def own_sums(w, p):
     ww = total(w * w)
     wp = total(w * p)
-    q = jnp.where(ww > 0, wp / jnp.where(ww > 0, ww, 1.0), 0.0)
+    q = quotient_of(ww, wp)
     d = p - q * w
-    return d, (ww, wp, total(d * d), q)
+    return ww, wp, total(d * d), q
+
+
+def write_payload(out_ref, w, p):
+    q = quotient_of(total(w * w), total(w * p)).astype(BF16).astype(F32)
+    out_ref[pl.ds(0, HALF), :] = (p - q * w).astype(BF16)
+    out_ref[pl.ds(HALF, TAIL), :] = jnp.broadcast_to(q, (TAIL, TILE)).astype(BF16)
 
 
 def merge(notes):
@@ -68,7 +79,7 @@
 
 
 def prepare_kernel(place, tiles_ref, pair_ref, couple_ref, left_ref, psi_ref,
-                   meta_ref, panel_ref, packed_ref, first):
+                   meta_ref, panel_ref, packed_ref, rounded_ref, first):
     sectors, channels = pair_ref.shape
     mine, core, channel = place[0], place[1], place[2]
 
@@ -86,7 +97,9 @@
     count = jnp.where(couple_ref[sector, channel] == 1, tiles_ref[source] * TILE, 0)
     column = lax.broadcasted_iota(jnp.int32, left_ref.shape, 1)
     panel_ref[...] = jnp.where(column < count, left_ref[...], jnp.zeros((), BF16))
-    packed_ref[...] = pack(psi_ref[...])
+    packed = pack(psi_ref[...].T)
+    packed_ref[...] = packed
+    rounded_ref[...] = packed.astype(BF16)
 
 
 def prepare(place, sector_tiles, pairing, coupling, left, psi):
@@ -94,11 +107,12 @@
     return pl.pallas_call(
         prepare_kernel,
         in_specs=[smem()] * 4 + [vmem()] * 2,
-        out_specs=[smem(), vmem(), vmem()],
+        out_specs=[smem(), vmem(), vmem(), vmem()],
         out_shape=[
             jax.ShapeDtypeStruct((channels + 1,), jnp.int32),
             jax.ShapeDtypeStruct(left.shape, BF16),
-            jax.ShapeDtypeStruct((psi.shape[0] // 2, psi.shape[1] * 2), F32),
+            jax.ShapeDtypeStruct((psi.shape[1] // 2, psi.shape[0] * 2), F32),
+            jax.ShapeDtypeStruct((psi.shape[1] // 2, psi.shape[0] * 2), BF16),
         ],
         scratch_shapes=[pltpu.SMEM(sector_tiles.shape, jnp.int32)],
         compiler_params=pltpu.CompilerParams(**PARAMS),
@@ -106,52 +120,59 @@
     )(place, sector_tiles, pairing, coupling, left, psi)
 
 
-def operator_kernel(turn, rows, width, *refs):
+def operator_kernel(turn, width, *refs):
     refs = list(refs)
-    meta = refs.pop(0)
-    vectors = [(refs.pop(0), refs.pop(0)) for _ in range(turn + 1)]
+    meta, start_ref = refs.pop(0), refs.pop(0)
+    arrived = [refs.pop(0) for _ in range(turn)]
     earlier = [refs.pop(0) for _ in range(turn)]
     note_ref = refs.pop(0) if turn == 2 else None
     panel_ref, right_ref, out_ref, rows_scr, mix_scr, acc, note_scr = refs
     step = pl.program_id(0)
-    pairs = rows // TILE // 2
+    tiles = start_ref.shape[0]
+    rows = tiles * TILE
     span = panel_ref.shape[2]
+    wide = rows_scr.shape[1]
+
+    def received(index):
+        d = arrived[index][:, pl.ds(0, HALF), :].astype(F32)
+        q = arrived[index][:, pl.ds(HALF, TAIL), :].astype(F32)[:, 0:1, 0:1]
+        return d, q
 
     @pl.when(step == 0)
     def _():
-        def both(index):
-            return [ref[...] for ref in vectors[index]]
-
-        if turn == 0:
-            d = both(0)
-        else:
-            w, p = both(0), both(1)
+        if turn > 0:
+            w = start_ref[...].astype(F32)
+            d, tile_q = received(0)
             if turn == 2:
                 q0, s0 = note_ref[0:1, 0:1], note_ref[0:1, 1:2]
-                w = [s0 * (b - q0 * a) for a, b in zip(w, p)]
-                p = both(2)
-            ww = total(w[0] * w[0] + w[1] * w[1])
-            wp = total(w[0] * p[0] + w[1] * p[1])
-            q = jnp.where(ww > 0, wp / jnp.where(ww > 0, ww, 1.0), 0.0)
-            d = [b - q * a for a, b in zip(w, p)]
-            rr = total(d[0] * d[0] + d[1] * d[1])
-            note_scr[...] = lanes_of(ww, wp, rr, q)
-        core = meta[meta.shape[0] - 1]
-        for side in range(2):
-            u = d[side].astype(BF16)
-            parity = core if side == 0 else 1 - core
-            for z in range(pairs):
-                block = u[z * HALF : (z + 1) * HALF]
-                start = pl.multiple_of((2 * z + parity) * TILE, TILE)
-                rows_scr[pl.ds(start, HALF), :] = block[:, :width]
-                rows_scr[pl.ds(start + HALF, HALF), :] = block[:, width:]
-        rows_scr[pl.ds(rows, span), :] = jnp.zeros((span, width), BF16)
+                w = s0[None] * (d + (tile_q - q0[None]) * w)
+                d, tile_q = received(1)
+            p = d + tile_q * w
+            ww = total(jnp.sum(w * w, axis=0))
+            wp = total(jnp.sum(w * p, axis=0))
+            q = quotient_of(ww, wp)
+            rest = (tile_q - q[None]) * w
+            r = d + rest
+            note_scr[...] = lanes_of(ww, wp, total(jnp.sum(r * r, axis=0)), q)
+            rest = rest.astype(BF16)
+        for k in range(tiles):
+            source = start_ref if turn == 0 else arrived[turn - 1]
+            block = source[k, pl.ds(0, HALF), :]
+            low, high = block[:, :width], block[:, width:]
+            if turn > 0:
+                low = jnp.concatenate([low, rest[k][:, :width]], axis=1)
+                high = jnp.concatenate([high, rest[k][:, width:]], axis=1)
+            rows_scr[pl.ds(k * TILE, HALF), :] = low
+            rows_scr[pl.ds(k * TILE + HALF, HALF), :] = high
+        rows_scr[pl.ds(rows, span), :] = jnp.zeros((span, wide), BF16)
         acc[...] = jnp.zeros_like(acc)
 
     for i in range(GROUP):
         start = pl.multiple_of(meta[step * GROUP + i], TILE)
         slab = rows_scr[pl.ds(start, span), :]
         mixed = jnp.dot(panel_ref[i], slab, preferred_element_type=F32)
+        if turn > 0:
+            mixed = mixed[:, :width] + mixed[:, width:]
         mix_scr[:, i * width : (i + 1) * width] = mixed.astype(BF16)
     acc[...] += jnp.dot(mix_scr[...], right_ref[...], preferred_element_type=F32)
 
@@ -170,14 +191,14 @@
             out_ref[e, pl.ds(0, HALF), :] = packed
 
 
-def apply_operator(meta, vectors, earlier, note, panels, right):
+def apply_operator(meta, start, arrived, earlier, note, panels, right):
     turn = len(earlier)
     channels, tile, span = panels.shape
     full = right.shape[1]
     width = full // channels
-    rows = vectors[0][0].shape[0] * 4
+    rows = start.shape[0] * TILE
     whole = lambda shape: pl.BlockSpec(shape, lambda g, m: (0,) * len(shape))
-    args = [half for vector in vectors for half in vector] + list(earlier)
+    args = [start] + list(arrived) + list(earlier)
     if turn == 2:
         args.append(note)
     in_specs = [whole(a.shape) for a in args] + [
@@ -187,14 +208,14 @@
     args += [panels, right]
     out_shape = (channels, HALF + (NOTE if turn else 0), 2 * width)
     return pl.pallas_call(
-        functools.partial(operator_kernel, turn, rows, width),
+        functools.partial(operator_kernel, turn, width),
         grid_spec=pltpu.PrefetchScalarGridSpec(
             num_scalar_prefetch=1,
             grid=(channels // GROUP,),
             in_specs=in_specs,
             out_specs=whole(out_shape),
             scratch_shapes=[
-                pltpu.VMEM((rows + span, width), BF16),
+                pltpu.VMEM((rows + span, 2 * width if turn else width), BF16),
                 pltpu.VMEM((tile, GROUP * width), BF16),
                 pltpu.VMEM((tile, full), F32),
                 pltpu.VMEM((NOTE, TILE), F32),
@@ -208,7 +229,28 @@
     )(meta, *args)
 
 
-def settle_kernel(entries, last, arrived_ref, p_ref, w_ref, p_out, w_out, note_out, *rest):
+def open_kernel(arrived_ref, w_ref, p_out, payload_out):
+    p = jnp.sum(arrived_ref[...], axis=0)
+    p_out[...] = p
+    write_payload(payload_out, w_ref[...], p)
+
+
+def payload_shape():
+    return jax.ShapeDtypeStruct((HALF + TAIL, TILE), BF16)
+
+
+def open_settle(arrived, own_w):
+    return pl.pallas_call(
+        open_kernel,
+        in_specs=[vmem()] * 2,
+        out_specs=[vmem()] * 2,
+        out_shape=[jax.ShapeDtypeStruct(own_w.shape, F32), payload_shape()],
+        compiler_params=pltpu.CompilerParams(**PARAMS),
+        name="open_settle",
+    )(arrived, own_w)
+
+
+def settle_kernel(entries, last, arrived_ref, p_ref, w_ref, p_out, w_out, note_out, rest_out):
     _, _, energy, q = merge(arrived_ref[:, HALF, :])
     scale = lax.rsqrt(energy / entries + EPSILON)
     summed = jnp.sum(arrived_ref[:, pl.ds(0, HALF), :], axis=0)
@@ -218,15 +260,17 @@
     w_out[...] = w
     note_out[...] = lanes_of(q, scale)
     if last:
-        _, sums = own_sums(w, p)
-        rest[0][...] = jnp.broadcast_to(lanes_of(*sums)[None], rest[0].shape)
+        sums = lanes_of(*own_sums(w, p))
+        rest_out[...] = jnp.broadcast_to(sums[None], rest_out.shape)
+    else:
+        write_payload(rest_out, w, p)
 
 
 def settle(entries, last, arrived, own_p, own_w):
     block = jax.ShapeDtypeStruct(own_p.shape, F32)
     outs = [block, block, jax.ShapeDtypeStruct((NOTE, TILE), F32)]
-    if last:
-        outs.append(jax.ShapeDtypeStruct((arrived.shape[0], NOTE, TILE), F32))
+    notes = jax.ShapeDtypeStruct((arrived.shape[0], NOTE, TILE), F32)
+    outs.append(notes if last else payload_shape())
     return pl.pallas_call(
         functools.partial(settle_kernel, entries, last),
         in_specs=[vmem()] * 3,
@@ -259,23 +303,24 @@
     _, _, energy, q = merge(notes)
     scale = lax.rsqrt(energy / entries + EPSILON)
     p = product_refs[ITERS - 1][...]
-    next_out[...] = unpack(scale * (p - q * w_ref[...]))
+    next_out[...] = unpack(scale * (p - q * w_ref[...])).T
     for n in range(ITERS):
-        products_out[n] = unpack(product_refs[n][...])
-    quotients_out[...] = lanes_of(note0_ref[0:1, 0:1], note1_ref[0:1, 0:1], q)
+        products_out[n] = unpack(product_refs[n][...]).T
+    for n, value in enumerate((note0_ref[0:1, 0:1], note1_ref[0:1, 0:1], q)):
+        quotients_out[n] = value[0, 0]
 
 
 def finish(entries, own, other, w, notes, products, tile, width):
     outs = [
-        jax.ShapeDtypeStruct((ITERS, tile, width), F32),
-        jax.ShapeDtypeStruct((tile, width), F32),
-        jax.ShapeDtypeStruct((NOTE, TILE), F32),
+        jax.ShapeDtypeStruct((ITERS, width, tile), F32),
+        jax.ShapeDtypeStruct((width, tile), F32),
+        jax.ShapeDtypeStruct((ITERS,), F32),
     ]
     args = [own, other, w, *notes, *products]
     return pl.pallas_call(
         functools.partial(finish_kernel, entries),
         in_specs=[vmem()] * len(args),
-        out_specs=[vmem()] * 3,
+        out_specs=[vmem(), vmem(), smem()],
         out_shape=outs,
         name="finish",
     )(*args)
@@ -289,9 +334,10 @@
     return lax.all_to_all(x, axes, 0, 0, tiled=True)
 
 
-def gather_rows(packed):
-    own = lax.all_gather(packed, "z", axis=0, tiled=True)
-    return own, swap(own)
+def gather_rows(block):
+    tiles = lax.axis_size(("z", "c"))
+    rows = lax.all_gather(block, ("z", "c"), axis=0, tiled=True)
+    return rows.reshape((tiles,) + block.shape)
 
 
 def per_device(psi, env_left, env_right, sector_tiles, pairing, coupling):
@@ -302,11 +348,11 @@
     entries = float(tile * z_count * 2 * full_width)
     core = lax.axis_index("c")
     place = jnp.stack([lax.axis_index(("z", "c")), core, lax.axis_index(ENV)]).astype(jnp.int32)
-    meta, panel, own_w = prepare(
-        place, sector_tiles, pairing, coupling, env_left.reshape(tile, -1), psi
+    meta, panel, own_w, rounded = prepare(
+        place, sector_tiles, pairing, coupling, env_left.reshape(tile, -1), psi.T
     )
     panels = lax.all_gather(panel, ENV, axis=0)
-    w = gather_rows(own_w)
+    start = gather_rows(rounded)
 
     part = width // 2
     held = env_right.reshape(env_count, 2, part, full_width)
@@ -319,13 +365,15 @@
         jnp.stack([right_other, right_own], axis=1),
     ).reshape(full_width, full_width)
 
-    sent0 = apply_operator(meta, [w], [], None, panels, right)
-    p0_own = jnp.sum(exchange(sent0, ENV), axis=0)
-    p0 = gather_rows(p0_own)
-    sent1 = apply_operator(meta, [w, p0], [sent0], None, panels, right)
-    p1_own, w1_own, note0 = settle(entries, False, exchange(sent1, ENV), p0_own, own_w)
-    p1 = gather_rows(p1_own)
-    sent2 = apply_operator(meta, [w, p0, p1], [sent0, sent1], note0, panels, right)
+    sent0 = apply_operator(meta, start, [], [], None, panels, right)
+    p0_own, payload = open_settle(exchange(sent0, ENV), own_w)
+    d0 = gather_rows(payload)
+    sent1 = apply_operator(meta, start, [d0], [sent0], None, panels, right)
+    p1_own, w1_own, note0, payload = settle(
+        entries, False, exchange(sent1, ENV), p0_own, own_w
+    )
+    d1 = gather_rows(payload)
+    sent2 = apply_operator(meta, start, [d0, d1], [sent0, sent1], note0, panels, right)
     p2_own, w2_own, note1, notes = settle(
         entries, True, exchange(sent2, ENV), p1_own, w1_own
     )
@@ -334,7 +382,7 @@
     products, next_vector, quotients = finish(
         entries, got, swap(got), w2_own, [note0, note1], [p0_own, p1_own, p2_own], tile, width
     )
-    return (products, quotients[0, :ITERS], next_vector)
+    return (jnp.swapaxes(products, 1, 2), quotients, next_vector.T)
 
 
 def solution(mesh):

time: 286 us -> 268 us (0.937)
  starting transfers between devices: 40.8 us -> 11.6 us
  blocking collectives: 178 us -> 201 us
  local copies, waits for them, and re-layouts: 17 us -> 7.4 us
    ppermute x5 -> x2, starting transfers between devices: 40.8 us -> 11.6 us  [swap(): return lax.ppermute(x, 'c', [(0, 1), (1, 0)])]
    all_gather x3, blocking collectives: 82.7 us -> 105 us  [gather_rows(): rows = lax.all_gather(block, ('z', 'c'), axis=0, tiled=True)]
    unnamed x41 -> x32, local copies, waits for them, and re-layouts: 15.7 us -> 7.3 us
    ppermute x5 -> x2, waiting for transfers between devices: 3.91 us -> 0.88 us  [swap(): return lax.ppermute(x, 'c', [(0, 1), (1, 0)])]
    pallas_call x3 -> x4, Pallas kernels: 18.9 us -> 19.2 us  [the longest x3 19 us: apply_operator(): pl.pallas_call(functools.partial(operator_kernel, turn, width), grid_spec...]
  transfers between devices with their start and end apart: 6 -> 3, of which waited for: 3 -> 2; matrix products, arithmetic and copies ran while one was open for 1% -> 2% of each run, Pallas kernels for 0% -> 0%
where the time goes in v3:
time: 268 us; the launch traced here: 267 us
  blocking collectives  201 us (75%)
  Pallas kernels  26.1 us (10%)
  between operations  14.2 us (5%)
  starting transfers between devices  11.6 us (4%)
  local copies, waits for them, and re-layouts  7.4 us (3%)
  other arithmetic  4.08 us (2%)
    all_gather x3, blocking collectives, gather_rows(): rows = lax.all_gather(block, ('z', 'c'), axis=0, tiled=True)  105 us
    all_to_all x6, blocking collectives, exchange(): return lax.all_to_all(x, axes, 0, 0, tiled=True)  96 us
    pallas_call x3, Pallas kernels, apply_operator(): pl.pallas_call(functools.partial(operator_kernel, turn, width), grid_spec...  19 us
    ppermute x2, starting transfers between devices, swap(): return lax.ppermute(x, 'c', [(0, 1), (1, 0)])  11.6 us
    unnamed x32, local copies, waits for them, and re-layouts  7.3 us
  transfers between devices with their start and end apart: 3, of which 2 were waited for; matrix products, arithmetic and copies ran while one was open for 2% of the time, Pallas kernels for 0%

profile of v3, /device:TPU:1, one launch (start us, length us, event | category | flops | bytes accessed | tf_op | source)
XLA Modules:
  0.0 266.6 jit_solution(2430534568715533230)
XLA Ops:
  7.3 1.1 copy-done.3
  8.4 0.8 copy-done.6
  9.1 0.7 copy-done.10
  11.2 1.8 prepare.1
  13.1 22.2 %all_to_all.30 = bf16[16,32,1024]{2,1,0:T(8,128)(2,1)} all-to-all(bf16[16,32,1024]{2,1,0:T(8,128)(2,1)S(1)} %dynamic-slice_bitcast_fusion), channel_id=1, replica_groups=mesh['z'=16,'c'=2,'y'=4,'x'=4] {'y','x'}, dimensions={0} | all-to-all | bytes 2097152 | tf_op jit(solution)/shard_map/all_to_all | solution.py:334
  35.3 5.4 %collective-permute-start = (bf16[16,32,1024]{2,1,0:T(8,128)(2,1)}, bf16[16,32,1024]{2,1,0:T(8,128)(2,1)}, u32[]{:S(2)}, u32[]{:S(2)}) collective-permute-start(bf16[16,32,1024]{2,1,0:T(8,128)(2,1)} %all_to_all.30), channel_id=1, source_target_pairs={{0,16},{16,0},{1,17},{17,1},{2,18},{18,2},{3,19},{19,3},{4,20},{20... | collective-permute-start | bytes 3145736 | tf_op jit(solution)/shard_map/ppermute | solution.py:330
  40.7 38.9 %all_gather.15 = bf16[2048,128]{1,0:T(8,128)(2,1)S(1)} all-gather(bf16[64,128]{1,0:T(8,128)(2,1)S(1)} %get-tuple-element.21), channel_id=1, replica_groups=mesh['z'=16,'c'=2,'y'=4,'x'=4] {'z','c'}, dimensions={0}, use_global_device_ids=true | all-gather | bytes 540672 | tf_op jit(solution)/shard_map/all_gather | solution.py:339
  79.6 4.0 %maximum_select_fusion = bf16[16,2,32,1024]{3,2,1,0:T(8,128)(2,1)} fusion(bf16[16,1,32,1024]{3,2,1,0:T(8,128)(2,1)} %bitcast.10, bf16[16,1,32,1024]{3,2,1,0:T(8,128)(2,1)} %bitcast.9, pred[]{:T(512)S(6)} %eq.3), kind=kLoop, calls=%fused_computation | loop fusion | flops 3145728 | bytes 4194305 | tf_op jit(solution)/shard_map/jit(_where)/select_n | solution.py:362
  83.6 1.4 all-gather.3.cloned.1.call-done
  85.0 1.6 copy-done.1
  86.6 5.7 %operator_0.1.refs_3_.refs_4_ = f32[16,64,128]{2,1,0:T(8,128)S(1)} custom-call(s32[17]{0:T(128)S(1)} %get-tuple-element.20.refs_0_, bf16[32,64,128]{2,1,0:T(8,128)(2,1)S(1)} %bitcast.21, bf16[16,128,1024]{2,1,0:T(8,128)(2,1)} %bitcast.29, bf16[1024,1024]{1,0:T(8,128)(2,1)S(1)} %bitcast.18), custom_call_target="tpu_custom_call" | custom-call | tf_op jit(solution)/shard_map/operator_0/pallas_call | solution.py:210
  92.4 15.5 %all_to_all.31.arrived_ref = f32[16,64,128]{2,1,0:T(8,128)S(1)} all-to-all(f32[16,64,128]{2,1,0:T(8,128)S(1)} %operator_0.1.refs_3_.refs_4_), channel_id=1, replica_groups=mesh['z'=16,'c'=2,'y'=4,'x'=4] {'y','x'}, dimensions={0} | all-to-all | bytes 1048576 | tf_op jit(solution)/shard_map/all_to_all | solution.py:334
  108.0 34.6 %all_gather.18 = bf16[2560,128]{1,0:T(8,128)(2,1)S(1)} all-gather(bf16[80,128]{1,0:T(8,128)(2,1)S(1)} %get-tuple-element.24), channel_id=1, replica_groups=mesh['z'=16,'c'=2,'y'=4,'x'=4] {'z','c'}, dimensions={0}, use_global_device_ids=true | all-gather | bytes 675840 | tf_op jit(solution)/shard_map/all_gather | solution.py:339
  142.6 6.5 %operator_1.1.refs_5_ = f32[16,72,128]{2,1,0:T(8,128)S(1)} custom-call(s32[17]{0:T(128)S(1)} %get-tuple-element.20.refs_0_, bf16[32,64,128]{2,1,0:T(8,128)(2,1)S(1)} %bitcast.22, bf16[32,80,128]{2,1,0:T(8,128)(2,1)S(1)} %bitcast.24, f32[16,64,128]{2,1,0:T(8,128)S(1)} %operator_0.1.refs_3_.refs_4_, bf16[16,128,1024]{2,1,0:T(8,128)(2,1)} %bitcast.30, ...), custom_call_target="tpu_custom_call" | custom-call | tf_op jit(solution)/shard_map/operator_1/pallas_call | solution.py:210
  149.1 14.3 %all_to_all.32.arrived_ref = f32[16,72,128]{2,1,0:T(8,128)S(1)} all-to-all(f32[16,72,128]{2,1,0:T(8,128)S(1)} %operator_1.1.refs_5_), channel_id=1, replica_groups=mesh['z'=16,'c'=2,'y'=4,'x'=4] {'y','x'}, dimensions={0} | all-to-all | bytes 1179648 | tf_op jit(solution)/shard_map/all_to_all | solution.py:334
  163.9 31.4 %all_gather.19 = bf16[2560,128]{1,0:T(8,128)(2,1)S(1)} all-gather(bf16[80,128]{1,0:T(8,128)(2,1)S(1)} %get-tuple-element.26), channel_id=1, replica_groups=mesh['z'=16,'c'=2,'y'=4,'x'=4] {'z','c'}, dimensions={0}, use_global_device_ids=true | all-gather | bytes 675840 | tf_op jit(solution)/shard_map/all_gather | solution.py:339
  195.2 6.8 %operator_2.1 = f32[16,72,128]{2,1,0:T(8,128)S(1)} custom-call(s32[17]{0:T(128)S(1)} %get-tuple-element.20.refs_0_, bf16[32,64,128]{2,1,0:T(8,128)(2,1)S(1)} %bitcast.23, bf16[32,80,128]{2,1,0:T(8,128)(2,1)S(1)} %bitcast.25, bf16[32,80,128]{2,1,0:T(8,128)(2,1)S(1)} %bitcast.26, f32[16,64,128]{2,1,0:T(8,128)S(1)} %operator_0.1.refs_3_.refs_4_, ...), custom_call_target="tpu_custom_call" | custom-call | tf_op jit(solution)/shard_map/operator_2/pallas_call | solution.py:210
  202.0 14.5 %all_to_all.33.arrived_ref = f32[16,72,128]{2,1,0:T(8,128)S(1)} all-to-all(f32[16,72,128]{2,1,0:T(8,128)S(1)} %operator_2.1), channel_id=1, replica_groups=mesh['z'=16,'c'=2,'y'=4,'x'=4] {'y','x'}, dimensions={0} | all-to-all | bytes 1179648 | tf_op jit(solution)/shard_map/all_to_all | solution.py:334
  218.4 9.7 %all_to_all.34.got_ref = f32[16,8,128]{2,1,0:T(8,128)} all-to-all(f32[16,8,128]{2,1,0:T(8,128)S(1)} %get-tuple-element.30), channel_id=1, replica_groups=mesh['z'=16,'c'=2,'y'=4,'x'=4] {'y','x'}, dimensions={0} | all-to-all | bytes 131072 | tf_op jit(solution)/shard_map/all_to_all | solution.py:334
  228.1 1.9 combine.1
  230.0 20.0 %all_to_all.35.own_ref = f32[16,8,128]{2,1,0:T(8,128)S(1)} all-to-all(f32[16,8,128]{2,1,0:T(8,128)} %combine.1), channel_id=1, replica_groups=mesh['z'=16,'c'=2,'y'=4,'x'=4] {'z'}, dimensions={0} | all-to-all | bytes 131072 | tf_op jit(solution)/shard_map/all_to_all | solution.py:334
  250.0 6.2 %collective-permute-start.1 = (f32[16,8,128]{2,1,0:T(8,128)S(1)}, f32[16,8,128]{2,1,0:T(8,128)S(1)}, u32[]{:S(2)}, u32[]{:S(2)}) collective-permute-start(f32[16,8,128]{2,1,0:T(8,128)S(1)} %all_to_all.35.own_ref), channel_id=1, source_target_pairs={{0,16},{16,0},{1,17},{17,1},{2,18},{18,2},{3,19},{19,3},{4,20},{20... | collective-permute-start | bytes 196616 | tf_op jit(solution)/shard_map/ppermute | solution.py:330
  256.1 0.9 collective-permute-done.1.other_ref
  257.6 2.1 finish.1
  (36 shorter events, 4.8 us)
Async XLA Ops:
  7.2 5.8 %copy-start = (bf16[1,1024,1024]{2,1,0:T(8,128)(2,1)S(1)}, bf16[1,1024,1024]{2,1,0:T(8,128)(2,1)}, u32[]{:S(2)}) copy-start(bf16[1,1024,1024]{2,1,0:T(8,128)(2,1)} %param.8) | copy-start | bytes 6291460
  7.2 77.8 %all-gather.3.cloned.1.call-start = ((), (), s32[]{:S(2)}) async-start(), calls=%async_computation.6 | async-start | bytes 4456448 | tf_op jit(solution)/shard_map/all_gather | solution.py:354
  7.3 1.1 copy-start.3
  8.4 0.8 copy-start.6
  9.1 0.7 copy-start.10
  9.8 0.7 copy-start.11
  10.5 0.7 copy-start.13
  35.3 44.4 %collective-permute-start = (bf16[16,32,1024]{2,1,0:T(8,128)(2,1)}, bf16[16,32,1024]{2,1,0:T(8,128)(2,1)}, u32[]{:S(2)}, u32[]{:S(2)}) collective-permute-start(bf16[16,32,1024]{2,1,0:T(8,128)(2,1)} %all_to_all.30), channel_id=1, source_target_pairs={{0,16},{16,0},{1,17},{17,1},{2,18},{18,2},{3,19},{19,3},{4,20},{20... | collective-permute-start | bytes 3145736 | tf_op jit(solution)/shard_map/ppermute | solution.py:330
  85.0 1.6 copy-start.1
  92.3 50.2 %copy-start.2 = (bf16[16,2,32,1024]{3,2,1,0:T(8,128)(2,1)S(1)}, bf16[16,2,32,1024]{3,2,1,0:T(8,128)(2,1)}, u32[]{:S(2)}) copy-start(bf16[16,2,32,1024]{3,2,1,0:T(8,128)(2,1)} %maximum_select_fusion) | copy-start | bytes 6291460
  108.0 55.3 %copy-start.4 = (f32[64,128]{1,0:T(8,128)}, f32[64,128]{1,0:T(8,128)S(1)}, u32[]{:S(2)}) copy-start(f32[64,128]{1,0:T(8,128)S(1)} %get-tuple-element.25.p_ref.refs_0_) | copy-start | bytes 98308
  163.9 38.2 %copy-start.9 = (f32[8,128]{1,0:T(8,128)}, f32[8,128]{1,0:T(8,128)S(1)}, u32[]{:S(2)}) copy-start(f32[8,128]{1,0:T(8,128)S(1)} %get-tuple-element.27.refs_6_.note0_ref) | copy-start | bytes 12292
  163.9 52.6 %copy-start.5 = (f32[64,128]{1,0:T(8,128)}, f32[64,128]{1,0:T(8,128)S(1)}, u32[]{:S(2)}) copy-start(f32[64,128]{1,0:T(8,128)S(1)} %get-tuple-element.28.p_ref.refs_1_) | copy-start | bytes 98308
  217.2 0.6 copy-start.7
  217.8 0.6 copy-start.8
  218.4 38.6 %copy-start.12 = (f32[8,128]{1,0:T(8,128)}, f32[8,128]{1,0:T(8,128)S(1)}, u32[]{:S(2)}) copy-start(f32[8,128]{1,0:T(8,128)S(1)} %get-tuple-element.32.note1_ref) | copy-start | bytes 12292
  249.9 7.1 %copy-start.14 = (f32[16,8,128]{2,1,0:T(8,128)}, f32[16,8,128]{2,1,0:T(8,128)S(1)}, u32[]{:S(2)}) copy-start(f32[16,8,128]{2,1,0:T(8,128)S(1)} %all_to_all.35.own_ref) | copy-start | bytes 196612
  250.0 7.0 %collective-permute-start.1 = (f32[16,8,128]{2,1,0:T(8,128)S(1)}, f32[16,8,128]{2,1,0:T(8,128)S(1)}, u32[]{:S(2)}, u32[]{:S(2)}) collective-permute-start(f32[16,8,128]{2,1,0:T(8,128)S(1)} %all_to_all.35.own_ref), channel_id=1, source_target_pairs={{0,16},{16,0},{1,17},{17,1},{2,18},{18,2},{3,19},{19,3},{4,20},{20... | collective-permute-start | bytes 196616 | tf_op jit(solution)/shard_map/ppermute | solution.py:330
  257.0 0.6 copy-start.15
Sparse Core Ops, SparseCore 0:
  13.1 71.8 all-gather.2

commit v4 on v3

--- a/solution.py
+++ b/solution.py
@@ -11,7 +11,7 @@
 TILE = 128
 HALF = TILE // 2
 ITERS = 3
-GROUP = 4
+GROUP = 8
 NOTE = 8
 TAIL = 16
 
@@ -126,8 +126,8 @@
     arrived = [refs.pop(0) for _ in range(turn)]
     earlier = [refs.pop(0) for _ in range(turn)]
     note_ref = refs.pop(0) if turn == 2 else None
-    panel_ref, right_ref, out_ref, rows_scr, mix_scr, acc, note_scr = refs
-    step = pl.program_id(0)
+    panels_ref, right_ref, out_ref, rows_scr, panel_ref, mix_scr, acc, note_scr, sems = refs
+    channels = panel_ref.shape[0]
     tiles = start_ref.shape[0]
     rows = tiles * TILE
     span = panel_ref.shape[2]
@@ -138,57 +138,62 @@
         q = arrived[index][:, pl.ds(HALF, TAIL), :].astype(F32)[:, 0:1, 0:1]
         return d, q
 
-    @pl.when(step == 0)
-    def _():
+    copies = []
+    for g in range(channels // GROUP):
+        part = pl.ds(g * GROUP, GROUP)
+        copies.append(
+            pltpu.make_async_copy(panels_ref.at[part], panel_ref.at[part], sems.at[g])
+        )
+        copies[g].start()
+
+    if turn > 0:
+        w = start_ref[...].astype(F32)
+        d, tile_q = received(0)
+        if turn == 2:
+            q0, s0 = note_ref[0:1, 0:1], note_ref[0:1, 1:2]
+            w = s0[None] * (d + (tile_q - q0[None]) * w)
+            d, tile_q = received(1)
+        p = d + tile_q * w
+        ww = total(jnp.sum(w * w, axis=0))
+        wp = total(jnp.sum(w * p, axis=0))
+        q = quotient_of(ww, wp)
+        rest = (tile_q - q[None]) * w
+        r = d + rest
+        note_scr[...] = lanes_of(ww, wp, total(jnp.sum(r * r, axis=0)), q)
+        rest = rest.astype(BF16)
+    for k in range(tiles):
+        source = start_ref if turn == 0 else arrived[turn - 1]
+        block = source[k, pl.ds(0, HALF), :]
+        low, high = block[:, :width], block[:, width:]
         if turn > 0:
-            w = start_ref[...].astype(F32)
-            d, tile_q = received(0)
+            low = jnp.concatenate([low, rest[k][:, :width]], axis=1)
+            high = jnp.concatenate([high, rest[k][:, width:]], axis=1)
+        rows_scr[pl.ds(k * TILE, HALF), :] = low
+        rows_scr[pl.ds(k * TILE + HALF, HALF), :] = high
+    rows_scr[pl.ds(rows, span), :] = jnp.zeros((span, wide), BF16)
+
+    for t in range(channels):
+        if t % GROUP == 0:
+            copies[t // GROUP].wait()
+        start = pl.multiple_of(meta[t], TILE)
+        slab = rows_scr[pl.ds(start, span), :]
+        mixed = jnp.dot(panel_ref[t], slab, preferred_element_type=F32)
+        if turn > 0:
+            mixed = mixed[:, :width] + mixed[:, width:]
+        mix_scr[:, t * width : (t + 1) * width] = mixed.astype(BF16)
+    acc[...] = jnp.dot(mix_scr[...], right_ref[...], preferred_element_type=F32)
+
+    for e in range(out_ref.shape[0]):
+        cols = acc[:, e * width : (e + 1) * width]
+        packed = jnp.concatenate([cols[:HALF], cols[HALF:]], axis=1)
+        if turn > 0:
+            before = earlier[0][e, pl.ds(0, HALF), :]
             if turn == 2:
                 q0, s0 = note_ref[0:1, 0:1], note_ref[0:1, 1:2]
-                w = s0[None] * (d + (tile_q - q0[None]) * w)
-                d, tile_q = received(1)
-            p = d + tile_q * w
-            ww = total(jnp.sum(w * w, axis=0))
-            wp = total(jnp.sum(w * p, axis=0))
-            q = quotient_of(ww, wp)
-            rest = (tile_q - q[None]) * w
-            r = d + rest
-            note_scr[...] = lanes_of(ww, wp, total(jnp.sum(r * r, axis=0)), q)
-            rest = rest.astype(BF16)
-        for k in range(tiles):
-            source = start_ref if turn == 0 else arrived[turn - 1]
-            block = source[k, pl.ds(0, HALF), :]
-            low, high = block[:, :width], block[:, width:]
-            if turn > 0:
-                low = jnp.concatenate([low, rest[k][:, :width]], axis=1)
-                high = jnp.concatenate([high, rest[k][:, width:]], axis=1)
-            rows_scr[pl.ds(k * TILE, HALF), :] = low
-            rows_scr[pl.ds(k * TILE + HALF, HALF), :] = high
-        rows_scr[pl.ds(rows, span), :] = jnp.zeros((span, wide), BF16)
-        acc[...] = jnp.zeros_like(acc)
-
-    for i in range(GROUP):
-        start = pl.multiple_of(meta[step * GROUP + i], TILE)
-        slab = rows_scr[pl.ds(start, span), :]
-        mixed = jnp.dot(panel_ref[i], slab, preferred_element_type=F32)
-        if turn > 0:
-            mixed = mixed[:, :width] + mixed[:, width:]
-        mix_scr[:, i * width : (i + 1) * width] = mixed.astype(BF16)
-    acc[...] += jnp.dot(mix_scr[...], right_ref[...], preferred_element_type=F32)
-
-    @pl.when(step == pl.num_programs(0) - 1)
-    def _():
-        for e in range(out_ref.shape[0]):
-            cols = acc[:, e * width : (e + 1) * width]
-            packed = jnp.concatenate([cols[:HALF], cols[HALF:]], axis=1)
-            if turn > 0:
-                before = earlier[0][e, pl.ds(0, HALF), :]
-                if turn == 2:
-                    q0, s0 = note_ref[0:1, 0:1], note_ref[0:1, 1:2]
-                    before = s0 * (earlier[1][e, pl.ds(0, HALF), :] - q0 * before)
-                packed = packed + note_scr[0:1, 3:4] * before
-                out_ref[e, pl.ds(HALF, NOTE), :] = note_scr[...]
-            out_ref[e, pl.ds(0, HALF), :] = packed
+                before = s0 * (earlier[1][e, pl.ds(0, HALF), :] - q0 * before)
+            packed = packed + note_scr[0:1, 3:4] * before
+            out_ref[e, pl.ds(HALF, NOTE), :] = note_scr[...]
+        out_ref[e, pl.ds(0, HALF), :] = packed
 
 
 def apply_operator(meta, start, arrived, earlier, note, panels, right):
@@ -197,36 +202,26 @@
     full = right.shape[1]
     width = full // channels
     rows = start.shape[0] * TILE
-    whole = lambda shape: pl.BlockSpec(shape, lambda g, m: (0,) * len(shape))
     args = [start] + list(arrived) + list(earlier)
     if turn == 2:
         args.append(note)
-    in_specs = [whole(a.shape) for a in args] + [
-        pl.BlockSpec((GROUP, tile, span), lambda g, m: (g, 0, 0)),
-        pl.BlockSpec((GROUP * width, full), lambda g, m: (g, 0)),
-    ]
-    args += [panels, right]
     out_shape = (channels, HALF + (NOTE if turn else 0), 2 * width)
     return pl.pallas_call(
         functools.partial(operator_kernel, turn, width),
-        grid_spec=pltpu.PrefetchScalarGridSpec(
-            num_scalar_prefetch=1,
-            grid=(channels // GROUP,),
-            in_specs=in_specs,
-            out_specs=whole(out_shape),
-            scratch_shapes=[
-                pltpu.VMEM((rows + span, 2 * width if turn else width), BF16),
-                pltpu.VMEM((tile, GROUP * width), BF16),
-                pltpu.VMEM((tile, full), F32),
-                pltpu.VMEM((NOTE, TILE), F32),
-            ],
-        ),
+        in_specs=[smem()] + [vmem()] * len(args) + [pl.BlockSpec(memory_space=pl.ANY), vmem()],
+        out_specs=vmem(),
+        scratch_shapes=[
+            pltpu.VMEM((rows + span, 2 * width if turn else width), BF16),
+            pltpu.VMEM(panels.shape, BF16),
+            pltpu.VMEM((tile, full), BF16),
+            pltpu.VMEM((tile, full), F32),
+            pltpu.VMEM((NOTE, TILE), F32),
+            pltpu.SemaphoreType.DMA((channels // GROUP,)),
+        ],
         out_shape=jax.ShapeDtypeStruct(out_shape, F32),
-        compiler_params=pltpu.CompilerParams(
-            dimension_semantics=("arbitrary",), **PARAMS
-        ),
+        compiler_params=pltpu.CompilerParams(**PARAMS),
         name=f"operator_{turn}",
-    )(meta, *args)
+    )(meta, *args, panels, right)
 
 
 def open_kernel(arrived_ref, w_ref, p_out, payload_out):

time: 268 us -> 262 us (0.978)
  Pallas kernels: 26.1 us -> 21.1 us
    pallas_call x3, Pallas kernels: 19 us -> 14 us  [apply_operator(): pl.pallas_call(functools.partial(operator_kernel, turn, width), in_specs=...]
where the time goes in v4:
time: 262 us
  blocking collectives  201 us (77%)
  Pallas kernels  21.1 us (8%)
  between operations  14.2 us (5%)
  starting transfers between devices  11.6 us (4%)
  local copies, waits for them, and re-layouts  7.4 us (3%)
  other arithmetic  4.08 us (2%)
    all_gather x3, blocking collectives, gather_rows(): rows = lax.all_gather(block, ('z', 'c'), axis=0, tiled=True)  105 us
    all_to_all x6, blocking collectives, exchange(): return lax.all_to_all(x, axes, 0, 0, tiled=True)  96 us
    pallas_call x3, Pallas kernels, apply_operator(): pl.pallas_call(functools.partial(operator_kernel, turn, width), in_specs=...  14 us
    ppermute x2, starting transfers between devices, swap(): return lax.ppermute(x, 'c', [(0, 1), (1, 0)])  11.6 us
    unnamed x32, local copies, waits for them, and re-layouts  7.3 us
  transfers between devices with their start and end apart: 3, of which 2 were waited for; matrix products, arithmetic and copies ran while one was open for 2% of the time, Pallas kernels for 0%

profile of v4, /device:TPU:1, one launch (start us, length us, event | category | flops | bytes accessed | tf_op | source)
XLA Modules:
  0.0 261.6 jit_solution(6912137921788523543)
XLA Ops:
  7.3 1.1 copy-done.3
  8.4 0.8 copy-done.6
  9.1 0.7 copy-done.10
  11.2 1.8 prepare.1
  13.1 22.2 %all_to_all.30 = bf16[16,32,1024]{2,1,0:T(8,128)(2,1)} all-to-all(bf16[16,32,1024]{2,1,0:T(8,128)(2,1)S(1)} %dynamic-slice_bitcast_fusion), channel_id=1, replica_groups=mesh['z'=16,'c'=2,'y'=4,'x'=4] {'y','x'}, dimensions={0} | all-to-all | bytes 2097152 | tf_op jit(solution)/shard_map/all_to_all | solution.py:329
  35.3 5.4 %collective-permute-start = (bf16[16,32,1024]{2,1,0:T(8,128)(2,1)}, bf16[16,32,1024]{2,1,0:T(8,128)(2,1)}, u32[]{:S(2)}, u32[]{:S(2)}) collective-permute-start(bf16[16,32,1024]{2,1,0:T(8,128)(2,1)} %all_to_all.30), channel_id=1, source_target_pairs={{0,16},{16,0},{1,17},{17,1},{2,18},{18,2},{3,19},{19,3},{4,20},{20... | collective-permute-start | bytes 3145736 | tf_op jit(solution)/shard_map/ppermute | solution.py:325
  40.7 38.9 %all_gather.15 = bf16[2048,128]{1,0:T(8,128)(2,1)S(1)} all-gather(bf16[64,128]{1,0:T(8,128)(2,1)S(1)} %get-tuple-element.21), channel_id=1, replica_groups=mesh['z'=16,'c'=2,'y'=4,'x'=4] {'z','c'}, dimensions={0}, use_global_device_ids=true | all-gather | bytes 540672 | tf_op jit(solution)/shard_map/all_gather | solution.py:334
  79.6 4.0 %maximum_select_fusion = bf16[16,2,32,1024]{3,2,1,0:T(8,128)(2,1)} fusion(bf16[16,1,32,1024]{3,2,1,0:T(8,128)(2,1)} %bitcast.10, bf16[16,1,32,1024]{3,2,1,0:T(8,128)(2,1)} %bitcast.9, pred[]{:T(512)S(6)} %eq.3), kind=kLoop, calls=%fused_computation | loop fusion | flops 3145728 | bytes 4194305 | tf_op jit(solution)/shard_map/jit(_where)/select_n | solution.py:357
  83.6 1.4 all-gather.3.cloned.1.call-done
  85.0 1.6 copy-done.1
  86.6 4.3 %operator_0.1.refs_3_.refs_4_ = f32[16,64,128]{2,1,0:T(8,128)S(1)} custom-call(s32[17]{0:T(128)S(1)} %get-tuple-element.20.refs_0_, bf16[32,64,128]{2,1,0:T(8,128)(2,1)S(1)} %bitcast.21, bf16[16,128,1024]{2,1,0:T(8,128)(2,1)} %bitcast.29, bf16[1024,1024]{1,0:T(8,128)(2,1)S(1)} %bitcast.18), custom_call_target="tpu_custom_call" | custom-call | tf_op jit(solution)/shard_map/operator_0/pallas_call | solution.py:209
  90.9 15.5 %all_to_all.31.arrived_ref = f32[16,64,128]{2,1,0:T(8,128)S(1)} all-to-all(f32[16,64,128]{2,1,0:T(8,128)S(1)} %operator_0.1.refs_3_.refs_4_), channel_id=1, replica_groups=mesh['z'=16,'c'=2,'y'=4,'x'=4] {'y','x'}, dimensions={0} | all-to-all | bytes 1048576 | tf_op jit(solution)/shard_map/all_to_all | solution.py:329
  106.6 34.6 %all_gather.18 = bf16[2560,128]{1,0:T(8,128)(2,1)S(1)} all-gather(bf16[80,128]{1,0:T(8,128)(2,1)S(1)} %get-tuple-element.24), channel_id=1, replica_groups=mesh['z'=16,'c'=2,'y'=4,'x'=4] {'z','c'}, dimensions={0}, use_global_device_ids=true | all-gather | bytes 675840 | tf_op jit(solution)/shard_map/all_gather | solution.py:334
  141.2 4.7 %operator_1.1.refs_5_ = f32[16,72,128]{2,1,0:T(8,128)S(1)} custom-call(s32[17]{0:T(128)S(1)} %get-tuple-element.20.refs_0_, bf16[32,64,128]{2,1,0:T(8,128)(2,1)S(1)} %bitcast.22, bf16[32,80,128]{2,1,0:T(8,128)(2,1)S(1)} %bitcast.24, f32[16,64,128]{2,1,0:T(8,128)S(1)} %operator_0.1.refs_3_.refs_4_, bf16[16,128,1024]{2,1,0:T(8,128)(2,1)} %bitcast.30, ...), custom_call_target="tpu_custom_call" | custom-call | tf_op jit(solution)/shard_map/operator_1/pallas_call | solution.py:209
  145.9 14.3 %all_to_all.32.arrived_ref = f32[16,72,128]{2,1,0:T(8,128)S(1)} all-to-all(f32[16,72,128]{2,1,0:T(8,128)S(1)} %operator_1.1.refs_5_), channel_id=1, replica_groups=mesh['z'=16,'c'=2,'y'=4,'x'=4] {'y','x'}, dimensions={0} | all-to-all | bytes 1179648 | tf_op jit(solution)/shard_map/all_to_all | solution.py:329
  160.7 31.4 %all_gather.19 = bf16[2560,128]{1,0:T(8,128)(2,1)S(1)} all-gather(bf16[80,128]{1,0:T(8,128)(2,1)S(1)} %get-tuple-element.26), channel_id=1, replica_groups=mesh['z'=16,'c'=2,'y'=4,'x'=4] {'z','c'}, dimensions={0}, use_global_device_ids=true | all-gather | bytes 675840 | tf_op jit(solution)/shard_map/all_gather | solution.py:334
  192.0 5.0 %operator_2.1 = f32[16,72,128]{2,1,0:T(8,128)S(1)} custom-call(s32[17]{0:T(128)S(1)} %get-tuple-element.20.refs_0_, bf16[32,64,128]{2,1,0:T(8,128)(2,1)S(1)} %bitcast.23, bf16[32,80,128]{2,1,0:T(8,128)(2,1)S(1)} %bitcast.25, bf16[32,80,128]{2,1,0:T(8,128)(2,1)S(1)} %bitcast.26, f32[16,64,128]{2,1,0:T(8,128)S(1)} %operator_0.1.refs_3_.refs_4_, ...), custom_call_target="tpu_custom_call" | custom-call | tf_op jit(solution)/shard_map/operator_2/pallas_call | solution.py:209
  197.0 14.4 %all_to_all.33.arrived_ref = f32[16,72,128]{2,1,0:T(8,128)S(1)} all-to-all(f32[16,72,128]{2,1,0:T(8,128)S(1)} %operator_2.1), channel_id=1, replica_groups=mesh['z'=16,'c'=2,'y'=4,'x'=4] {'y','x'}, dimensions={0} | all-to-all | bytes 1179648 | tf_op jit(solution)/shard_map/all_to_all | solution.py:329
  213.4 9.7 %all_to_all.34.got_ref = f32[16,8,128]{2,1,0:T(8,128)} all-to-all(f32[16,8,128]{2,1,0:T(8,128)S(1)} %get-tuple-element.30), channel_id=1, replica_groups=mesh['z'=16,'c'=2,'y'=4,'x'=4] {'y','x'}, dimensions={0} | all-to-all | bytes 131072 | tf_op jit(solution)/shard_map/all_to_all | solution.py:329
  223.1 1.9 combine.1
  225.0 20.0 %all_to_all.35.own_ref = f32[16,8,128]{2,1,0:T(8,128)S(1)} all-to-all(f32[16,8,128]{2,1,0:T(8,128)} %combine.1), channel_id=1, replica_groups=mesh['z'=16,'c'=2,'y'=4,'x'=4] {'z'}, dimensions={0} | all-to-all | bytes 131072 | tf_op jit(solution)/shard_map/all_to_all | solution.py:329
  245.0 6.2 %collective-permute-start.1 = (f32[16,8,128]{2,1,0:T(8,128)S(1)}, f32[16,8,128]{2,1,0:T(8,128)S(1)}, u32[]{:S(2)}, u32[]{:S(2)}) collective-permute-start(f32[16,8,128]{2,1,0:T(8,128)S(1)} %all_to_all.35.own_ref), channel_id=1, source_target_pairs={{0,16},{16,0},{1,17},{17,1},{2,18},{18,2},{3,19},{19,3},{4,20},{20... | collective-permute-start | bytes 196616 | tf_op jit(solution)/shard_map/ppermute | solution.py:325
  251.1 0.9 collective-permute-done.1.other_ref
  252.6 2.1 finish.1
  (36 shorter events, 4.8 us)
Async XLA Ops:
  7.2 5.8 %copy-start = (bf16[1,1024,1024]{2,1,0:T(8,128)(2,1)S(1)}, bf16[1,1024,1024]{2,1,0:T(8,128)(2,1)}, u32[]{:S(2)}) copy-start(bf16[1,1024,1024]{2,1,0:T(8,128)(2,1)} %param.8) | copy-start | bytes 6291460
  7.2 77.8 %all-gather.3.cloned.1.call-start = ((), (), s32[]{:S(2)}) async-start(), calls=%async_computation.6 | async-start | bytes 4456448 | tf_op jit(solution)/shard_map/all_gather | solution.py:349
  7.3 1.1 copy-start.3
  8.4 0.8 copy-start.6
  9.1 0.7 copy-start.10
  9.8 0.7 copy-start.11
  10.5 0.7 copy-start.13
  35.3 44.4 %collective-permute-start = (bf16[16,32,1024]{2,1,0:T(8,128)(2,1)}, bf16[16,32,1024]{2,1,0:T(8,128)(2,1)}, u32[]{:S(2)}, u32[]{:S(2)}) collective-permute-start(bf16[16,32,1024]{2,1,0:T(8,128)(2,1)} %all_to_all.30), channel_id=1, source_target_pairs={{0,16},{16,0},{1,17},{17,1},{2,18},{18,2},{3,19},{19,3},{4,20},{20... | collective-permute-start | bytes 3145736 | tf_op jit(solution)/shard_map/ppermute | solution.py:325
  85.0 1.6 copy-start.1
  90.9 50.2 %copy-start.2 = (bf16[16,2,32,1024]{3,2,1,0:T(8,128)(2,1)S(1)}, bf16[16,2,32,1024]{3,2,1,0:T(8,128)(2,1)}, u32[]{:S(2)}) copy-start(bf16[16,2,32,1024]{3,2,1,0:T(8,128)(2,1)} %maximum_select_fusion) | copy-start | bytes 6291460
  106.6 53.6 %copy-start.4 = (f32[64,128]{1,0:T(8,128)}, f32[64,128]{1,0:T(8,128)S(1)}, u32[]{:S(2)}) copy-start(f32[64,128]{1,0:T(8,128)S(1)} %get-tuple-element.25.p_ref.refs_0_) | copy-start | bytes 98308
  160.7 36.4 %copy-start.9 = (f32[8,128]{1,0:T(8,128)}, f32[8,128]{1,0:T(8,128)S(1)}, u32[]{:S(2)}) copy-start(f32[8,128]{1,0:T(8,128)S(1)} %get-tuple-element.27.refs_6_.note0_ref) | copy-start | bytes 12292
  160.7 50.8 %copy-start.5 = (f32[64,128]{1,0:T(8,128)}, f32[64,128]{1,0:T(8,128)S(1)}, u32[]{:S(2)}) copy-start(f32[64,128]{1,0:T(8,128)S(1)} %get-tuple-element.28.p_ref.refs_1_) | copy-start | bytes 98308
  212.2 0.6 copy-start.7
  212.8 0.6 copy-start.8
  213.4 38.6 %copy-start.12 = (f32[8,128]{1,0:T(8,128)}, f32[8,128]{1,0:T(8,128)S(1)}, u32[]{:S(2)}) copy-start(f32[8,128]{1,0:T(8,128)S(1)} %get-tuple-element.32.note1_ref) | copy-start | bytes 12292
  245.0 7.1 %copy-start.14 = (f32[16,8,128]{2,1,0:T(8,128)}, f32[16,8,128]{2,1,0:T(8,128)S(1)}, u32[]{:S(2)}) copy-start(f32[16,8,128]{2,1,0:T(8,128)S(1)} %all_to_all.35.own_ref) | copy-start | bytes 196612
  245.0 7.0 %collective-permute-start.1 = (f32[16,8,128]{2,1,0:T(8,128)S(1)}, f32[16,8,128]{2,1,0:T(8,128)S(1)}, u32[]{:S(2)}, u32[]{:S(2)}) collective-permute-start(f32[16,8,128]{2,1,0:T(8,128)S(1)} %all_to_all.35.own_ref), channel_id=1, source_target_pairs={{0,16},{16,0},{1,17},{17,1},{2,18},{18,2},{3,19},{19,3},{4,20},{20... | collective-permute-start | bytes 196616 | tf_op jit(solution)/shard_map/ppermute | solution.py:325
  252.0 0.6 copy-start.15
Sparse Core Ops, SparseCore 0:
  13.1 71.8 all-gather.2
